TPU v7x, 128 devices: a whole 4x4x4 slice. The times are simulated.
128 devices in a mesh: gx: 8 (over z, x_lo), gy: 16 (over x_hi, y, core).
Axes of the slice: x: 4 (x_hi: 2, x_lo: 2; x = x_hi * 2 + x_lo), y: 4, z: 4, core: 2. Of those that a mesh axis runs over, the one named last changes fastest.
Arguments:
- fields: float32 [6, 256, 512, 128], P(None, 'gx', 'gy'), may hold values from -6 to 6
- eps_background: float32 [256, 512, 128], P('gx', 'gy'), may hold values from 1 to 4
- target: float32 [256, 256], replicated, may hold values from 1 to 10
- widths: float32 [16384], P(('gx', 'gy')), may hold values from 0.2 to 1
- intersection: float32 [16384, 16], P(('gx', 'gy')), may hold values from 0.1 to 1
- pillar_tile: int32 [16384, 1], P(('gx', 'gy')), may hold values from 0 to 127; in each aligned block of 128 rows (0 to 127, 128 to 255, ...) at most 2 rows name the same one
- anchors: int32 [16384, 2], P(('gx', 'gy')), may hold values from 0 to 28
Outputs:
- final_fields: float32 [6, 256, 512, 128], P(None, 'gx', 'gy')
- focal_power: float32 [256, 256], P(('gx', 'gy'))
- grad_widths: float32 [16384], P(('gx', 'gy'))
Inputs may be any that keep to these rules, and one draw needn't show every extreme that they name: `pillar_tile`: in the pillars of one device (aligned blocks of 128), no tile is named by more than 2 pillars, a bound that some block reaches. Tile t is the one at gx index t div (512 div 32) and gy index t mod (512 div 32).
All inputs are finite; a program needn't handle non-finite values.
Results may differ from a plain program's by a relative error of at most 0.00016.
Values sent between devices are 32-bit elements; how exact they have to be, the bound alone decides.
A program may use at most 128 MiB of HBM per device.

v0:
```python
import math

import jax
import jax.numpy as jnp
from jax import lax
from jax.sharding import PartitionSpec as P
from jax.experimental import pallas as pl
from jax.experimental.pallas import tpu as pltpu

TILE = 32
P_DEV = 128
NT = 4
ZP = 4
U = 256
V = 256
ZM = 64


COURANT = 0.5
ANGULAR_STEP = 0.9
DELTA_EPS = 4.0


def passed_along(shard, axis, by):
    count = lax.axis_size(axis)
    pairs = [(i, i + by) for i in range(count) if 0 <= i + by < count]
    return lax.ppermute(shard, axis, pairs)


def plus_diff(field, rim_layer, axis):
    extended = jnp.concatenate([field, rim_layer], axis=axis)
    return lax.slice_in_dim(extended, 1, extended.shape[axis], axis=axis) - field


def minus_diff(field, rim_layer, axis):
    extended = jnp.concatenate([rim_layer, field], axis=axis)
    return field - lax.slice_in_dim(extended, 0, field.shape[axis], axis=axis)


def leap_step(fields_now, inv_eps, sources):
    elec_x, elec_y, elec_z, magn_x, magn_y, magn_z = fields_now
    z_blank = jnp.zeros_like(elec_x[:, :, :1])
    rim_east = passed_along(jnp.stack([elec_y[:1], elec_z[:1]]), "gx", -1)
    rim_north = passed_along(jnp.stack([elec_x[:, :1], elec_z[:, :1]]), "gy", -1)
    curl_x = plus_diff(elec_z, rim_north[1], 1) - plus_diff(elec_y, z_blank, 2)
    curl_y = plus_diff(elec_x, z_blank, 2) - plus_diff(elec_z, rim_east[1], 0)
    curl_z = plus_diff(elec_y, rim_east[0], 0) - plus_diff(elec_x, rim_north[0], 1)
    magn_x = magn_x - COURANT * curl_x
    magn_y = magn_y - COURANT * curl_y
    magn_z = magn_z - COURANT * curl_z
    rim_west = passed_along(jnp.stack([magn_y[-1:], magn_z[-1:]]), "gx", 1)
    rim_south = passed_along(jnp.stack([magn_x[:, -1:], magn_z[:, -1:]]), "gy", 1)
    curl_x = minus_diff(magn_z, rim_south[1], 1) - minus_diff(magn_y, z_blank, 2)
    curl_y = minus_diff(magn_x, z_blank, 2) - minus_diff(magn_z, rim_west[1], 0)
    curl_z = minus_diff(magn_y, rim_west[0], 0) - minus_diff(magn_x, rim_south[0], 1)
    elec_x = elec_x + COURANT * (curl_x - sources[0]) * inv_eps
    elec_y = elec_y + COURANT * (curl_y - sources[1]) * inv_eps
    elec_z = elec_z + COURANT * curl_z * inv_eps
    return (elec_x, elec_y, elec_z, magn_x, magn_y, magn_z)


def run_leaps(e_start, h_start, inv_eps, drive, tag):
    span_x = lax.axis_size("gx")
    span_y = lax.axis_size("gy")
    size_x, size_y, size_z = inv_eps.shape
    zero_start = e_start is None
    with_drive = drive is not None
    mesh_id = pl.DeviceIdType.MESH

    def kernel(*refs):
        refs = list(refs)
        if zero_start:
            e_in = h_in = None
        else:
            e_in, h_in = refs.pop(0), refs.pop(0)
        eps_ref = refs.pop(0)
        drv = refs.pop(0) if with_drive else None
        e_out, h_out, east, north, west, south, xs_e, ys_e, xs_h, ys_h, ssem, rsem = refs
        px = lax.axis_index("gx")
        py = lax.axis_index("gy")
        barrier = pltpu.get_barrier_semaphore()
        for peer in (
            (lax.rem(px + 1, span_x), py),
            (lax.rem(px + span_x - 1, span_x), py),
            (px, lax.rem(py + 1, span_y)),
            (px, lax.rem(py + span_y - 1, span_y)),
        ):
            pl.semaphore_signal(barrier, 1, device_id=peer, device_id_type=mesh_id)
        pl.semaphore_wait(barrier, 4)
        has_east = px < span_x - 1
        has_west = px > 0
        has_north = py < span_y - 1
        has_south = py > 0
        zero_slab = jnp.zeros((size_y, size_z), jnp.float32)
        iy = lax.broadcasted_iota(jnp.int32, (size_y, size_z), 0)
        iz = lax.broadcasted_iota(jnp.int32, (size_y, size_z), 1)

        def up_y(slab, row):
            return jnp.where(iy == size_y - 1, row, pltpu.roll(slab, size_y - 1, 0))

        def down_y(slab, row):
            return jnp.where(iy == 0, row, pltpu.roll(slab, 1, 0))

        def up_z(slab):
            return jnp.where(iz == size_z - 1, 0.0, pltpu.roll(slab, size_z - 1, 1))

        def down_z(slab):
            return jnp.where(iz == 0, 0.0, pltpu.roll(slab, 1, 1))

        def load_e(step, comp, x):
            if step == 0:
                return zero_slab if zero_start else e_in[comp, x]
            return e_out[step - 1, comp, x]

        def load_h(step, comp, x):
            if step == 0:
                return zero_slab if zero_start else h_in[comp, x]
            return h_out[comp, x]

        def swap(src_x, dst_x, src_y, dst_y, sem, to_x, to_y, sends_x, sends_y, gets_x, gets_y):
            copy_x = pltpu.make_async_remote_copy(
                src_ref=src_x, dst_ref=dst_x, send_sem=ssem.at[sem], recv_sem=rsem.at[sem],
                device_id=(to_x, py), device_id_type=mesh_id,
            )
            copy_y = pltpu.make_async_remote_copy(
                src_ref=src_y, dst_ref=dst_y, send_sem=ssem.at[sem + 1], recv_sem=rsem.at[sem + 1],
                device_id=(px, to_y), device_id_type=mesh_id,
            )
            pl.when(sends_x)(copy_x.start)
            pl.when(sends_y)(copy_y.start)

            @pl.when(jnp.logical_not(gets_x))
            def _():
                dst_x[...] = jnp.zeros(dst_x.shape, jnp.float32)

            @pl.when(jnp.logical_not(gets_y))
            def _():
                dst_y[...] = jnp.zeros(dst_y.shape, jnp.float32)

            pl.when(gets_x)(copy_x.wait_recv)
            pl.when(gets_y)(copy_y.wait_recv)
            pl.when(sends_x)(copy_x.wait_send)
            pl.when(sends_y)(copy_y.wait_send)

        if not zero_start:
            xs_e[0, 0] = e_in[1, 0]
            xs_e[0, 1] = e_in[2, 0]

            def stage_first(x, carry):
                ys_e[0, 0, pl.ds(x, 1), :] = e_in[0, x][0:1, :]
                ys_e[0, 1, pl.ds(x, 1), :] = e_in[2, x][0:1, :]
                return carry

            lax.fori_loop(0, size_x, stage_first, 0)

        for step in range(NT):
            if step == 0 and zero_start:
                east[0] = jnp.zeros(east.shape[1:], jnp.float32)
                north[0] = jnp.zeros(north.shape[1:], jnp.float32)
            else:
                swap(
                    xs_e.at[step], east.at[step], ys_e.at[step], north.at[step], 4 * step,
                    lax.rem(px + span_x - 1, span_x), lax.rem(py + span_y - 1, span_y),
                    has_west, has_south, has_east, has_north,
                )

            def magnetic(x, ey_next, ez_next, step=step):
                ex = load_e(step, 0, x)
                ey = load_e(step, 1, x)
                ez = load_e(step, 2, x)
                nx_row = north[step, 0, pl.ds(x, 1), :]
                nz_row = north[step, 1, pl.ds(x, 1), :]
                curl_x = (up_y(ez, nz_row) - ez) - (up_z(ey) - ey)
                curl_y = (up_z(ex) - ex) - (ez_next - ez)
                curl_z = (ey_next - ey) - (up_y(ex, nx_row) - ex)
                hx = load_h(step, 0, x) - COURANT * curl_x
                hy = load_h(step, 1, x) - COURANT * curl_y
                hz = load_h(step, 2, x) - COURANT * curl_z
                h_out[0, x] = hx
                h_out[1, x] = hy
                h_out[2, x] = hz
                ys_h[step, 0, pl.ds(x, 1), :] = hx[size_y - 1 : size_y, :]
                ys_h[step, 1, pl.ds(x, 1), :] = hz[size_y - 1 : size_y, :]
                return hy, hz

            def magnetic_body(x, carry, step=step):
                magnetic(x, load_e(step, 1, x + 1), load_e(step, 2, x + 1))
                return carry

            lax.fori_loop(0, size_x - 1, magnetic_body, 0)
            hy_last, hz_last = magnetic(size_x - 1, east[step, 0], east[step, 1])
            xs_h[step, 0] = hy_last
            xs_h[step, 1] = hz_last
            swap(
                xs_h.at[step], west.at[step], ys_h.at[step], south.at[step], 4 * step + 2,
                lax.rem(px + 1, span_x), lax.rem(py + 1, span_y),
                has_east, has_north, has_west, has_south,
            )

            def electric(x, hy_prev, hz_prev, step=step):
                hx = h_out[0, x]
                hy = h_out[1, x]
                hz = h_out[2, x]
                sx_row = south[step, 0, pl.ds(x, 1), :]
                sz_row = south[step, 1, pl.ds(x, 1), :]
                curl_x = (hz - down_y(hz, sz_row)) - (hy - down_z(hy))
                curl_y = (hx - down_z(hx)) - (hz - hz_prev)
                curl_z = (hy - hy_prev) - (hx - down_y(hx, sx_row))
                if with_drive:
                    curl_x = curl_x - drv[step, 0, x]
                    curl_y = curl_y - drv[step, 1, x]
                scale = eps_ref[x]
                ex = load_e(step, 0, x) + COURANT * curl_x * scale
                ey = load_e(step, 1, x) + COURANT * curl_y * scale
                ez = load_e(step, 2, x) + COURANT * curl_z * scale
                e_out[step, 0, x] = ex
                e_out[step, 1, x] = ey
                e_out[step, 2, x] = ez
                if step + 1 < NT:
                    ys_e[step + 1, 0, pl.ds(x, 1), :] = ex[0:1, :]
                    ys_e[step + 1, 1, pl.ds(x, 1), :] = ez[0:1, :]
                return ey, ez

            ey_first, ez_first = electric(0, west[step, 0], west[step, 1])
            if step + 1 < NT:
                xs_e[step + 1, 0] = ey_first
                xs_e[step + 1, 1] = ez_first

            def electric_body(x, carry, step=step):
                electric(x, h_out[1, x - 1], h_out[2, x - 1])
                return carry

            lax.fori_loop(1, size_x, electric_body, 0)

    rim_x = pltpu.VMEM((NT, 2, size_y, size_z), jnp.float32)
    rim_y = pltpu.VMEM((NT, 2, size_x, size_z), jnp.float32)
    operands = ([] if zero_start else [e_start, h_start]) + [inv_eps] + ([drive] if with_drive else [])
    return pl.pallas_call(
        kernel,
        out_shape=(
            jax.ShapeDtypeStruct((NT, 3, size_x, size_y, size_z), jnp.float32),
            jax.ShapeDtypeStruct((3, size_x, size_y, size_z), jnp.float32),
        ),
        in_specs=[pl.BlockSpec(memory_space=pltpu.VMEM)] * len(operands),
        out_specs=(pl.BlockSpec(memory_space=pltpu.VMEM),) * 2,
        scratch_shapes=[
            rim_x, rim_y, rim_x, rim_y, rim_x, rim_y, rim_x, rim_y,
            pltpu.SemaphoreType.DMA((4 * NT,)),
            pltpu.SemaphoreType.DMA((4 * NT,)),
        ],
        compiler_params=pltpu.CompilerParams(
            collective_id=tag, has_side_effects=True, vmem_limit_bytes=48 * 1024 * 1024
        ),
    )(*operands)


def group_of(axes):
    sizes = [lax.axis_size(a) for a in axes]
    count = math.prod(sizes)
    return count, sizes


def group_place(axes, sizes):
    place = 0
    for axis, size in zip(axes, sizes):
        place = place * size + lax.axis_index(axis)
    return place


def group_device(axes, sizes, peer):
    coords = {}
    rest = peer
    for axis, size in reversed(list(zip(axes, sizes))):
        coords[axis] = rest % size
        rest = rest // size
    return tuple(coords[a] if a in coords else lax.axis_index(a) for a in ("gx", "gy"))


def exchange(pieces, axes, gather, tag):
    count, sizes = group_of(axes)
    piece_shape = pieces.shape if gather else pieces.shape[1:]

    def kernel(x_ref, o_ref, send_sem, recv_sem):
        me = group_place(axes, sizes)
        barrier = pltpu.get_barrier_semaphore()
        for step in range(1, count):
            peer = lax.rem(me + step, count)
            pl.semaphore_signal(
                barrier, 1, device_id=group_device(axes, sizes, peer),
                device_id_type=pl.DeviceIdType.MESH,
            )
        pl.semaphore_wait(barrier, count - 1)
        copies = []
        for step in range(1, count):
            peer = lax.rem(me + step, count)
            copy = pltpu.make_async_remote_copy(
                src_ref=x_ref if gather else x_ref.at[peer],
                dst_ref=o_ref.at[me],
                send_sem=send_sem.at[step],
                recv_sem=recv_sem.at[step],
                device_id=group_device(axes, sizes, peer),
                device_id_type=pl.DeviceIdType.MESH,
            )
            copy.start()
            copies.append(copy)
        own = x_ref[...] if gather else x_ref[me]
        o_ref[me] = own
        for copy in copies:
            copy.wait_send()
        for step in range(1, count):
            source = lax.rem(me + count - step, count)
            pltpu.make_async_remote_copy(
                src_ref=x_ref if gather else x_ref.at[source],
                dst_ref=o_ref.at[source],
                send_sem=send_sem.at[step],
                recv_sem=recv_sem.at[step],
                device_id=group_device(axes, sizes, source),
                device_id_type=pl.DeviceIdType.MESH,
            ).wait_recv()

    return pl.pallas_call(
        kernel,
        out_shape=jax.ShapeDtypeStruct((count,) + tuple(piece_shape), pieces.dtype),
        in_specs=[pl.BlockSpec(memory_space=pltpu.VMEM)],
        out_specs=pl.BlockSpec(memory_space=pltpu.VMEM),
        scratch_shapes=[pltpu.SemaphoreType.DMA((count,)), pltpu.SemaphoreType.DMA((count,))],
        compiler_params=pltpu.CompilerParams(collective_id=tag, has_side_effects=True),
    )(pieces)


def kernel_table(count_out, count_in, offset, length):
    focal_pos = (jnp.arange(count_out, dtype=jnp.float32) + 0.5) / count_out - 0.5
    cell_pos = (
        offset.astype(jnp.float32) + jnp.arange(length, dtype=jnp.float32) + 0.5
    ) / count_in - 0.5
    phase = math.pi * count_out * (focal_pos[:, None] - cell_pos[None, :]) ** 2
    return (jnp.cos(phase), jnp.sin(phase))


def contract(pattern, first_op, second_op):
    return jnp.einsum(pattern, first_op, second_op, precision=lax.Precision.HIGHEST)


def route_pillars(rows, slot_ids, devices, capacity):
    slots = devices * capacity
    placing = (slot_ids[:, None] == jnp.arange(slots, dtype=jnp.int32)[None, :]).astype(
        jnp.float32
    )
    packed = contract("ps,pk->sk", placing, rows)
    got = exchange(packed.reshape(devices, capacity, rows.shape[1]), ("gx", "gy"), False, 0)
    return placing, got.reshape(slots, rows.shape[1])


def shards(fields, eps_background, target, widths, intersection, pillar_tile, anchors):
    span_x = lax.axis_size("gx")
    span_y = lax.axis_size("gy")
    devices = span_x * span_y
    place_x = lax.axis_index("gx")
    place_y = lax.axis_index("gy")
    linear = place_x * span_y + place_y
    offsets = jnp.arange(16, dtype=jnp.int32)
    capacity = 2 * max(1, P_DEV // devices)
    target_tile = pillar_tile[:, 0]
    onehot = (target_tile[:, None] == jnp.arange(devices, dtype=jnp.int32)[None, :]).astype(
        jnp.int32
    )
    earlier = jnp.cumsum(onehot, axis=0) - onehot
    order_in = jnp.sum(earlier * onehot, axis=1)
    slot_ids = target_tile * capacity + order_in
    rows = jnp.concatenate(
        [intersection * widths[:, None], anchors.astype(jnp.float32)], axis=1
    )
    placing, got = route_pillars(rows, slot_ids, devices, capacity)
    local_vals = got[:, :16]
    local_at = got[:, 16:18].astype(jnp.int32)
    cells_x = (local_at[:, 0:1] + (offsets // 4)[None, :]).reshape(-1)
    cells_y = (local_at[:, 1:2] + (offsets % 4)[None, :]).reshape(-1)
    lanes = jnp.arange(TILE, dtype=jnp.int32)
    pick_x = (cells_x[:, None] == lanes[None, :]).astype(jnp.float32)
    pick_y = (cells_y[:, None] == lanes[None, :]).astype(jnp.float32)
    filling = contract("sx,sy->xy", pick_x, pick_y * local_vals.reshape(-1)[:, None])
    z_index = jnp.arange(fields.shape[3], dtype=jnp.int32)
    layers = ((z_index >= ZM - ZP) & (z_index < ZM)).astype(jnp.float32)
    permittivity = eps_background + DELTA_EPS * filling[:, :, None] * layers[None, None, :]
    inv_eps = 1.0 / permittivity
    fields_now = tuple((fields[component] for component in range(6)))
    e_steps, h_last = run_leaps(fields[:3], fields[3:], inv_eps, None, 10)
    mon_re = jnp.zeros((2, TILE, TILE), jnp.float32)
    mon_im = jnp.zeros((2, TILE, TILE), jnp.float32)
    changes = []
    before = fields[:3]
    for moment in range(1, NT + 1):
        after = e_steps[moment - 1]
        monitor = after[0:2, :, :, ZM]
        mon_re = mon_re + math.cos(ANGULAR_STEP * moment) * monitor
        mon_im = mon_im - math.sin(ANGULAR_STEP * moment) * monitor
        changes.append((after - before)[:, :, :, ZM - ZP : ZM])
        before = after
    norm_scale = (TILE * span_x * TILE * span_y) ** (-0.5)
    x_re, x_im = kernel_table(U, TILE * span_x, place_x * TILE, TILE)
    y_re, y_im = kernel_table(V, TILE * span_y, place_y * TILE, TILE)
    part = jnp.stack(
        [
            contract("ux,cxy->ucy", x_re, mon_re) - contract("ux,cxy->ucy", x_im, mon_im),
            contract("ux,cxy->ucy", x_re, mon_im) + contract("ux,cxy->ucy", x_im, mon_re),
        ]
    )
    chunk_u = U // span_x
    part = part.reshape(2, span_x, chunk_u, 2, TILE).transpose(1, 2, 0, 3, 4)
    part = exchange(part.reshape(span_x, chunk_u, 4 * TILE), ("gx",), False, 1)
    part = jnp.sum(part, axis=0).reshape(chunk_u, 2, 2, TILE)
    part_re, part_im = part[:, 0], part[:, 1]
    far = jnp.stack(
        [
            contract("ucy,vy->cuv", part_re, y_re) - contract("ucy,vy->cuv", part_im, y_im),
            contract("ucy,vy->cuv", part_re, y_im) + contract("ucy,vy->cuv", part_im, y_re),
        ],
        axis=2,
    )
    row_count = U // devices
    far = far.reshape(2, span_y, row_count, 2, V).transpose(1, 0, 2, 3, 4)
    far = exchange(far.reshape(span_y, 2 * row_count * 2, V), ("gy",), False, 2)
    far = norm_scale * jnp.sum(far, axis=0).reshape(2, row_count, 2, V)
    focal_power = jnp.sum(far * far, axis=(0, 2))
    mine_target = lax.dynamic_slice_in_dim(target, linear * row_count, row_count, 0)
    weighted = jnp.stack(
        [mine_target * far[:, :, 0], -(mine_target * far[:, :, 1])], axis=2
    )
    weighted = exchange(weighted.reshape(2 * row_count * 2, V), ("gy",), True, 3)
    weighted = weighted.reshape(span_y, 2, row_count, 2, V).transpose(1, 0, 2, 3, 4)
    weighted = weighted.reshape(2, span_y * row_count, 2, V)
    w_re, w_im = weighted[:, :, 0], weighted[:, :, 1]
    half = jnp.stack(
        [
            contract("cuv,vy->cuy", w_re, y_re) - contract("cuv,vy->cuy", w_im, y_im),
            contract("cuv,vy->cuy", w_re, y_im) + contract("cuv,vy->cuy", w_im, y_re),
        ]
    )
    half = half.transpose(2, 0, 1, 3).reshape(chunk_u, 4 * TILE)
    half = exchange(half, ("gx",), True, 4)
    half = half.reshape(span_x * chunk_u, 2, 2, TILE).transpose(1, 2, 0, 3)
    half_re, half_im = half[0], half[1]
    back_re = 2.0 * norm_scale * (
        contract("ux,cuy->cxy", x_re, half_re) - contract("ux,cuy->cxy", x_im, half_im)
    )
    back_im = 2.0 * norm_scale * (
        contract("ux,cuy->cxy", x_re, half_im) + contract("ux,cuy->cxy", x_im, half_re)
    )
    inv_layer = inv_eps[:, :, ZM - ZP : ZM]
    drives = []
    for moment in range(1, NT + 1):
        source_step = NT + 1 - moment
        adj_drive = (
            math.cos(ANGULAR_STEP * source_step) * back_re
            + math.sin(ANGULAR_STEP * source_step) * back_im
        )
        drives.append(adj_drive)
    drive = jnp.stack(drives)
    z_index = jnp.arange(fields.shape[3], dtype=jnp.int32)
    drive = jnp.where(z_index == ZM, drive[..., None], 0.0)
    a_steps, _ = run_leaps(None, None, inv_eps, drive, 11)
    grad_eps = jnp.zeros((TILE, TILE, ZP), jnp.float32)
    for moment in range(1, NT + 1):
        source_step = NT + 1 - moment
        change = changes[source_step - 1]
        adjoint = a_steps[moment - 1][:, :, :, ZM - ZP : ZM]
        product = adjoint[0] * change[0] + adjoint[1] * change[1] + adjoint[2] * change[2]
        grad_eps = grad_eps - product * inv_layer
    column_grad = jnp.sum(grad_eps, axis=2)
    spread = contract("sx,xy->sy", pick_x, column_grad)
    picked = jnp.sum(spread * pick_y, axis=1).reshape(devices * capacity, 16)
    returned = exchange(picked.reshape(devices, capacity, 16), ("gx", "gy"), False, 5)
    own_vals = contract("ps,sk->pk", placing, returned.reshape(devices * capacity, 16))
    grad_widths = DELTA_EPS * jnp.sum(intersection * own_vals, axis=1)
    return (jnp.concatenate([e_steps[NT - 1], h_last]), focal_power, grad_widths)


def solution(mesh):
    placed = (
        P(None, "gx", "gy", None),
        P("gx", "gy", None),
        P(),
        P(("gx", "gy")),
        P(("gx", "gy"), None),
        P(("gx", "gy"), None),
        P(("gx", "gy"), None),
    )
    return jax.shard_map(
        shards,
        mesh=mesh,
        in_specs=placed,
        out_specs=(P(None, "gx", "gy", None), P(("gx", "gy"), None), P(("gx", "gy"))),
        check_vma=False,
    )
```

profile of v0, /device:TPU:1, one launch (start us, length us, event | category | flops | bytes accessed | tf_op | source)
XLA Modules:
  0.0 252.0 jit_solution(8681290314834047361)
XLA Ops:
  4.7 1.0 fusion.34
  5.7 20.7 %shard_map.94 = f32[128,2,18]{2,1,0:T(2,128)} custom-call(f32[128,2,18]{2,1,0:T(2,128)} %bitcast.197), custom_call_target="tpu_custom_call" | custom-call | tf_op jit(solution)/shard_map/pallas_call | solution.py:321
  26.4 1.0 mul.255
  27.4 1.0 slice_convert_fusion
  29.7 2.5 fusion.155
  32.2 49.4 %shard_map.95 = (f32[4,3,32,32,128]{4,3,2,1,0:T(8,128)}, f32[3,32,32,128]{3,2,1,0:T(8,128)S(1)}) custom-call(f32[3,32,32,128]{3,2,1,0:T(8,128)S(1)} %get-tuple-element.26.refs_0_, f32[3,32,32,128]{3,2,1,0:T(8,128)S(1)} %get-tuple-element.25.refs_1_, f32[32,32,128]{2,1,0:T(8,128)S(1)} %add_divide_fusion.refs_2_.refs_0_), custom_call_target="tpu_custom_call" | custom-call | tf_op jit(solution)/shard_map/pallas_call | solution.py:238
  81.6 3.5 %slice_bitcast_fusion.6 = (f32[3,32,32,128]{3,2,1,0:T(8,128)S(1)}, f32[3,32,32,128]{3,2,1,0:T(8,128)S(1)}, f32[3,32,32,128]{3,2,1,0:T(8,128)S(1)}, f32[3,32,32,128]{3,2,1,0:T(8,128)S(1)}) fusion(f32[4,3,32,32,128]{4,3,2,1,0:T(8,128)} %get-tuple-element.6), kind=kLoop, calls=%fused_computation.9 | loop fusion | bytes 12582912 | tf_op jit(solution)/shard_map/squeeze | solution.py:393
  85.1 1.1 multiply_add_fusion
  86.3 2.2 pad_maximum_fusion
  89.1 6.5 %fusion.152 = (f32[3,32,32,128]{3,2,1,0:T(8,128)S(1)}, f32[3,32,32,128]{3,2,1,0:T(8,128)}, f32[3,32,32,128]{3,2,1,0:T(8,128)}, f32[3,32,32,128]{3,2,1,0:T(8,128)}) fusion(f32[4,3,32,32,128]{4,3,2,1,0:T(8,128)} %get-tuple-element.6, f32[6,32,32,128]{3,2,1,0:T(8,128)} %param.7), kind=kLoop, calls=%fused_computation.214 | loop fusion | flops 1572864 | bytes 14155776 | tf_op jit(solution)/shard_map/sub | solution.py:397
  98.4 1.1 reshape.182.x_ref
  99.4 9.0 %shard_map.96 = f32[8,32,128]{2,1,0:T(8,128)} custom-call(f32[8,32,128]{2,1,0:T(8,128)} %reshape.182.x_ref), custom_call_target="tpu_custom_call" | custom-call | tf_op jit(solution)/shard_map/pallas_call | solution.py:321
  112.1 22.9 %shard_map.97 = f32[16,8,256]{2,1,0:T(8,128)} custom-call(f32[16,8,256]{2,1,0:T(8,128)} %reshape.184.x_ref), custom_call_target="tpu_custom_call" | custom-call | tf_op jit(solution)/shard_map/pallas_call | solution.py:321
  135.1 0.9 reduce_sum.68
  137.2 9.4 %shard_map.98 = f32[16,8,256]{2,1,0:T(8,128)} custom-call(f32[8,256]{1,0:T(8,128)} %reshape.185.x_ref), custom_call_target="tpu_custom_call" | custom-call | tf_op jit(solution)/shard_map/pallas_call | solution.py:321
  146.7 1.0 reshape.186
  150.2 6.7 %shard_map.99 = f32[8,32,128]{2,1,0:T(8,128)} custom-call(f32[32,128]{1,0:T(8,128)} %reshape.188.x_ref), custom_call_target="tpu_custom_call" | custom-call | tf_op jit(solution)/shard_map/pallas_call | solution.py:321
  156.9 1.3 reshape.204
  160.4 2.7 %broadcast_select_fusion.refs_1_ = f32[4,2,32,32,128]{4,3,2,1,0:T(8,128)} fusion(f32[4,2,32,32]{3,2,1,0:T(8,128)S(1)} %copy.69, pred[128]{0:T(512)(128)(4,1)S(1)} %iota_compare_fusion.8), kind=kLoop, calls=%fused_computation.2 | loop fusion | flops 1048576 | bytes 4227200 | tf_op jit(solution)/shard_map/jit(_where)/select_n | solution.py:460
  163.0 48.9 %shard_map.100 = (f32[4,3,32,32,128]{4,3,2,1,0:T(8,128)}, f32[3,32,32,128]{3,2,1,0:T(8,128)}) custom-call(f32[32,32,128]{2,1,0:T(8,128)S(1)} %add_divide_fusion.refs_2_.refs_0_, f32[4,2,32,32,128]{4,3,2,1,0:T(8,128)} %broadcast_select_fusion.refs_1_), custom_call_target="tpu_custom_call" | custom-call | tf_op jit(solution)/shard_map/pallas_call | solution.py:238
  212.0 3.7 %slice_bitcast_fusion.3 = (f32[3,32,32,128]{3,2,1,0:T(8,128)S(1)}, f32[3,32,32,128]{3,2,1,0:T(8,128)S(1)}, f32[3,32,32,128]{3,2,1,0:T(8,128)S(1)}, f32[3,32,32,128]{3,2,1,0:T(8,128)S(1)}) fusion(f32[4,3,32,32,128]{4,3,2,1,0:T(8,128)} %get-tuple-element.8), kind=kLoop, calls=%fused_computation.6 | loop fusion | bytes 12582912 | tf_op jit(solution)/shard_map/squeeze | solution.py:466
  216.2 3.6 %fusion.10 = f32[32,32]{1,0:T(8,128)S(1)} fusion(f32[3,32,32,128]{3,2,1,0:T(8,128)S(1)} %copy-done.3, f32[3,32,32,128]{3,2,1,0:T(8,128)S(1)} %get-tuple-element.12, f32[3,32,32,128]{3,2,1,0:T(8,128)S(1)} %copy-done.2, f32[3,32,32,128]{3,2,1,0:T(8,128)S(1)} %get-tuple-element.13, f32[3,32,32,128]{3,2,1,0:T(8,128)S(1)} %copy-done.1, ...), kind=kLoop, calls=%fused_computation.32 | loop fusion | flops 117760 | bytes 413696 | tf_op jit(solution)/shard_map/reduce_sum | solution.py:469
  221.1 29.2 %shard_map.101 = f32[128,2,16]{2,1,0:T(2,128)} custom-call(f32[128,2,16]{2,1,0:T(2,128)} %reshape_reshape.3.x_ref), custom_call_target="tpu_custom_call" | custom-call | tf_op jit(solution)/shard_map/pallas_call | solution.py:321
  250.3 1.2 fusion.5
  (81 shorter events, 20.3 us)
Async XLA Ops:
  0.6 1.0 copy-start
  0.6 28.8 %copy-start.4 = (f32[32,32,128]{2,1,0:T(8,128)S(1)}, f32[32,32,128]{2,1,0:T(8,128)}, u32[]{:S(2)}) copy-start(f32[32,32,128]{2,1,0:T(8,128)} %param.8) | copy-start | bytes 1572868
  211.9 3.8 %copy-start.1 = (f32[3,32,32,128]{3,2,1,0:T(8,128)S(1)}, f32[3,32,32,128]{3,2,1,0:T(8,128)}, u32[]{:S(2)}) copy-start(f32[3,32,32,128]{3,2,1,0:T(8,128)} %get-tuple-element.16) | copy-start | bytes 4718596
  211.9 3.8 %copy-start.2 = (f32[3,32,32,128]{3,2,1,0:T(8,128)S(1)}, f32[3,32,32,128]{3,2,1,0:T(8,128)}, u32[]{:S(2)}) copy-start(f32[3,32,32,128]{3,2,1,0:T(8,128)} %get-tuple-element.17) | copy-start | bytes 4718596
  211.9 4.2 %copy-start.3 = (f32[3,32,32,128]{3,2,1,0:T(8,128)S(1)}, f32[3,32,32,128]{3,2,1,0:T(8,128)}, u32[]{:S(2)}) copy-start(f32[3,32,32,128]{3,2,1,0:T(8,128)} %get-tuple-element.18) | copy-start | bytes 4718596
  216.2 34.1 %copy-start.5 = (f32[128,16]{0,1:T(8,128)S(1)}, f32[128,16]{0,1:T(8,128)}, u32[]{:S(2)}) copy-start(f32[128,16]{0,1:T(8,128)} %param.11) | copy-start | bytes 24580
where the time goes:
time: 253 us; the launch traced here: 252 us
  Pallas kernels  196 us (77%)
  other arithmetic  24.8 us (10%)
  local copies, waits for them, and re-layouts  20.4 us (8%)
  matrix products  9.4 us (4%)
    pallas_call x2, Pallas kernels, run_leaps(): pl.pallas_call(kernel, out_shape=(jax.ShapeDtypeStruct((NT, 3, size_x, si...  98.2 us
    pallas_call x6, Pallas kernels, exchange(): pl.pallas_call(kernel, out_shape=jax.ShapeDtypeStruct((count,) + tuple(pi...  97.9 us
    dot_general x16, matrix products, contract(): jnp.einsum(pattern, first_op, second_op, precision=lax.Precision.HIGHEST)  7.9 us
    sub x1, other arithmetic, shards(): changes.append((after - before)[:, :, :, ZM - ZP:ZM])  6.48 us

commit v1 on v0

--- a/solution.py
+++ b/solution.py
@@ -187,7 +187,7 @@
                 magnetic(x, load_e(step, 1, x + 1), load_e(step, 2, x + 1))
                 return carry
 
-            lax.fori_loop(0, size_x - 1, magnetic_body, 0)
+            lax.fori_loop(0, size_x - 1, magnetic_body, 0, unroll=True)
             hy_last, hz_last = magnetic(size_x - 1, east[step, 0], east[step, 1])
             xs_h[step, 0] = hy_last
             xs_h[step, 1] = hz_last
@@ -230,7 +230,7 @@
                 electric(x, h_out[1, x - 1], h_out[2, x - 1])
                 return carry
 
-            lax.fori_loop(1, size_x, electric_body, 0)
+            lax.fori_loop(1, size_x, electric_body, 0, unroll=True)
 
     rim_x = pltpu.VMEM((NT, 2, size_y, size_z), jnp.float32)
     rim_y = pltpu.VMEM((NT, 2, size_x, size_z), jnp.float32)

time: 253 us -> 218 us (0.86)
  Pallas kernels: 196 us -> 161 us
    pallas_call x2, Pallas kernels: 98.2 us -> 63 us  [run_leaps(): pl.pallas_call(kernel, out_shape=(jax.ShapeDtypeStruct((NT, 3, size_x, si...]
where the time goes in v1:
time: 218 us; the launch traced here: 217 us
  Pallas kernels  161 us (74%)
  other arithmetic  24.8 us (11%)
  local copies, waits for them, and re-layouts  20.4 us (9%)
  matrix products  9.4 us (4%)
    pallas_call x6, Pallas kernels, exchange(): pl.pallas_call(kernel, out_shape=jax.ShapeDtypeStruct((count,) + tuple(pi...  98.3 us
    pallas_call x2, Pallas kernels, run_leaps(): pl.pallas_call(kernel, out_shape=(jax.ShapeDtypeStruct((NT, 3, size_x, si...  63 us
    dot_general x16, matrix products, contract(): jnp.einsum(pattern, first_op, second_op, precision=lax.Precision.HIGHEST)  7.9 us
    sub x1, other arithmetic, shards(): changes.append((after - before)[:, :, :, ZM - ZP:ZM])  6.48 us

profile of v1, /device:TPU:1, one launch (start us, length us, event | category | flops | bytes accessed | tf_op | source)
XLA Modules:
  0.0 217.1 jit_solution(8036023900061997611)
XLA Ops:
  4.7 1.0 fusion.34
  5.7 20.7 %shard_map.94 = f32[128,2,18]{2,1,0:T(2,128)} custom-call(f32[128,2,18]{2,1,0:T(2,128)} %bitcast.197), custom_call_target="tpu_custom_call" | custom-call | tf_op jit(solution)/shard_map/pallas_call | solution.py:321
  26.4 1.0 mul.255
  27.4 1.0 slice_convert_fusion
  29.7 2.5 %fusion.155 = (f32[3,32,32,128]{3,2,1,0:T(8,128)S(1)}, f32[3,32,32,128]{3,2,1,0:T(8,128)S(1)}) fusion(f32[6,32,32,128]{3,2,1,0:T(8,128)} %param.7), kind=kLoop, calls=%fused_computation.218 | loop fusion | bytes 6291456 | tf_op jit(solution)/shard_map/slice | solution.py:387
  32.2 31.9 %shard_map.95 = (f32[4,3,32,32,128]{4,3,2,1,0:T(8,128)}, f32[3,32,32,128]{3,2,1,0:T(8,128)S(1)}) custom-call(f32[3,32,32,128]{3,2,1,0:T(8,128)S(1)} %get-tuple-element.26.refs_0_, f32[3,32,32,128]{3,2,1,0:T(8,128)S(1)} %get-tuple-element.25.refs_1_, f32[32,32,128]{2,1,0:T(8,128)S(1)} %add_divide_fusion.refs_2_.refs_0_), custom_call_target="tpu_custom_call" | custom-call | tf_op jit(solution)/shard_map/pallas_call | solution.py:238
  64.1 3.5 %slice_bitcast_fusion.6 = (f32[3,32,32,128]{3,2,1,0:T(8,128)S(1)}, f32[3,32,32,128]{3,2,1,0:T(8,128)S(1)}, f32[3,32,32,128]{3,2,1,0:T(8,128)S(1)}, f32[3,32,32,128]{3,2,1,0:T(8,128)S(1)}) fusion(f32[4,3,32,32,128]{4,3,2,1,0:T(8,128)} %get-tuple-element.6), kind=kLoop, calls=%fused_computation.9 | loop fusion | bytes 12582912 | tf_op jit(solution)/shard_map/squeeze | solution.py:393
  67.6 1.1 multiply_add_fusion
  68.8 2.2 %pad_maximum_fusion = f32[6,32,32,128]{3,2,1,0:T(8,128)} fusion(f32[3,32,32,128]{3,2,1,0:T(8,128)S(1)} %get-tuple-element.7, f32[3,32,32,128]{3,2,1,0:T(8,128)S(1)} %get-tuple-element.24), kind=kLoop, calls=%fused_computation.1 | loop fusion | flops 786432 | bytes 6291456 | tf_op jit(solution)/shard_map/concatenate | solution.py:475
  71.7 6.5 %fusion.152 = (f32[3,32,32,128]{3,2,1,0:T(8,128)S(1)}, f32[3,32,32,128]{3,2,1,0:T(8,128)}, f32[3,32,32,128]{3,2,1,0:T(8,128)}, f32[3,32,32,128]{3,2,1,0:T(8,128)}) fusion(f32[4,3,32,32,128]{4,3,2,1,0:T(8,128)} %get-tuple-element.6, f32[6,32,32,128]{3,2,1,0:T(8,128)} %param.7), kind=kLoop, calls=%fused_computation.214 | loop fusion | flops 1572864 | bytes 14155776 | tf_op jit(solution)/shard_map/sub | solution.py:397
  80.9 1.1 reshape.182.x_ref
  82.0 9.3 %shard_map.96 = f32[8,32,128]{2,1,0:T(8,128)} custom-call(f32[8,32,128]{2,1,0:T(8,128)} %reshape.182.x_ref), custom_call_target="tpu_custom_call" | custom-call | tf_op jit(solution)/shard_map/pallas_call | solution.py:321
  95.0 23.0 %shard_map.97 = f32[16,8,256]{2,1,0:T(8,128)} custom-call(f32[16,8,256]{2,1,0:T(8,128)} %reshape.184.x_ref), custom_call_target="tpu_custom_call" | custom-call | tf_op jit(solution)/shard_map/pallas_call | solution.py:321
  118.1 0.9 reduce_sum.68
  120.3 9.4 %shard_map.98 = f32[16,8,256]{2,1,0:T(8,128)} custom-call(f32[8,256]{1,0:T(8,128)} %reshape.185.x_ref), custom_call_target="tpu_custom_call" | custom-call | tf_op jit(solution)/shard_map/pallas_call | solution.py:321
  129.7 1.0 reshape.186
  133.2 6.7 %shard_map.99 = f32[8,32,128]{2,1,0:T(8,128)} custom-call(f32[32,128]{1,0:T(8,128)} %reshape.188.x_ref), custom_call_target="tpu_custom_call" | custom-call | tf_op jit(solution)/shard_map/pallas_call | solution.py:321
  139.9 1.3 reshape.204
  143.4 2.7 %broadcast_select_fusion.refs_1_ = f32[4,2,32,32,128]{4,3,2,1,0:T(8,128)} fusion(f32[4,2,32,32]{3,2,1,0:T(8,128)S(1)} %copy.69, pred[128]{0:T(512)(128)(4,1)S(1)} %iota_compare_fusion.8), kind=kLoop, calls=%fused_computation.2 | loop fusion | flops 1048576 | bytes 4227200 | tf_op jit(solution)/shard_map/jit(_where)/select_n | solution.py:460
  146.1 31.1 %shard_map.100 = (f32[4,3,32,32,128]{4,3,2,1,0:T(8,128)}, f32[3,32,32,128]{3,2,1,0:T(8,128)}) custom-call(f32[32,32,128]{2,1,0:T(8,128)S(1)} %add_divide_fusion.refs_2_.refs_0_, f32[4,2,32,32,128]{4,3,2,1,0:T(8,128)} %broadcast_select_fusion.refs_1_), custom_call_target="tpu_custom_call" | custom-call | tf_op jit(solution)/shard_map/pallas_call | solution.py:238
  177.2 3.7 %slice_bitcast_fusion.3 = (f32[3,32,32,128]{3,2,1,0:T(8,128)S(1)}, f32[3,32,32,128]{3,2,1,0:T(8,128)S(1)}, f32[3,32,32,128]{3,2,1,0:T(8,128)S(1)}, f32[3,32,32,128]{3,2,1,0:T(8,128)S(1)}) fusion(f32[4,3,32,32,128]{4,3,2,1,0:T(8,128)} %get-tuple-element.8), kind=kLoop, calls=%fused_computation.6 | loop fusion | bytes 12582912 | tf_op jit(solution)/shard_map/squeeze | solution.py:466
  181.4 3.6 %fusion.10 = f32[32,32]{1,0:T(8,128)S(1)} fusion(f32[3,32,32,128]{3,2,1,0:T(8,128)S(1)} %copy-done.3, f32[3,32,32,128]{3,2,1,0:T(8,128)S(1)} %get-tuple-element.12, f32[3,32,32,128]{3,2,1,0:T(8,128)S(1)} %copy-done.2, f32[3,32,32,128]{3,2,1,0:T(8,128)S(1)} %get-tuple-element.13, f32[3,32,32,128]{3,2,1,0:T(8,128)S(1)} %copy-done.1, ...), kind=kLoop, calls=%fused_computation.32 | loop fusion | flops 117760 | bytes 413696 | tf_op jit(solution)/shard_map/reduce_sum | solution.py:469
  186.3 29.1 %shard_map.101 = f32[128,2,16]{2,1,0:T(2,128)} custom-call(f32[128,2,16]{2,1,0:T(2,128)} %reshape_reshape.3.x_ref), custom_call_target="tpu_custom_call" | custom-call | tf_op jit(solution)/shard_map/pallas_call | solution.py:321
  215.4 1.2 fusion.5
  (81 shorter events, 20.3 us)
Async XLA Ops:
  0.6 1.0 copy-start
  0.6 28.8 %copy-start.4 = (f32[32,32,128]{2,1,0:T(8,128)S(1)}, f32[32,32,128]{2,1,0:T(8,128)}, u32[]{:S(2)}) copy-start(f32[32,32,128]{2,1,0:T(8,128)} %param.8) | copy-start | bytes 1572868
  177.2 3.8 %copy-start.1 = (f32[3,32,32,128]{3,2,1,0:T(8,128)S(1)}, f32[3,32,32,128]{3,2,1,0:T(8,128)}, u32[]{:S(2)}) copy-start(f32[3,32,32,128]{3,2,1,0:T(8,128)} %get-tuple-element.16) | copy-start | bytes 4718596
  177.2 3.8 %copy-start.2 = (f32[3,32,32,128]{3,2,1,0:T(8,128)S(1)}, f32[3,32,32,128]{3,2,1,0:T(8,128)}, u32[]{:S(2)}) copy-start(f32[3,32,32,128]{3,2,1,0:T(8,128)} %get-tuple-element.17) | copy-start | bytes 4718596
  177.2 4.2 %copy-start.3 = (f32[3,32,32,128]{3,2,1,0:T(8,128)S(1)}, f32[3,32,32,128]{3,2,1,0:T(8,128)}, u32[]{:S(2)}) copy-start(f32[3,32,32,128]{3,2,1,0:T(8,128)} %get-tuple-element.18) | copy-start | bytes 4718596
  181.4 34.0 %copy-start.5 = (f32[128,16]{0,1:T(8,128)S(1)}, f32[128,16]{0,1:T(8,128)}, u32[]{:S(2)}) copy-start(f32[128,16]{0,1:T(8,128)} %param.11) | copy-start | bytes 24580

commit v2 on v1

--- a/solution.py
+++ b/solution.py
@@ -328,6 +328,16 @@
     )(pieces)
 
 
+def route_tiles(pieces, tags):
+    span_x = lax.axis_size("gx")
+    span_y = lax.axis_size("gy")
+    tail = pieces.shape[1:]
+    staged = pieces.reshape((span_x, span_y) + tail).swapaxes(0, 1)
+    staged = exchange(staged, ("gy",), False, tags[0])
+    staged = exchange(staged.swapaxes(0, 1), ("gx",), False, tags[1])
+    return staged.reshape((span_x * span_y,) + tail)
+
+
 def kernel_table(count_out, count_in, offset, length):
     focal_pos = (jnp.arange(count_out, dtype=jnp.float32) + 0.5) / count_out - 0.5
     cell_pos = (
@@ -347,7 +357,7 @@
         jnp.float32
     )
     packed = contract("ps,pk->sk", placing, rows)
-    got = exchange(packed.reshape(devices, capacity, rows.shape[1]), ("gx", "gy"), False, 0)
+    got = route_tiles(packed.reshape(devices, capacity, rows.shape[1]), (0, 6))
     return placing, got.reshape(slots, rows.shape[1])
 
 
@@ -469,7 +479,7 @@
     column_grad = jnp.sum(grad_eps, axis=2)
     spread = contract("sx,xy->sy", pick_x, column_grad)
     picked = jnp.sum(spread * pick_y, axis=1).reshape(devices * capacity, 16)
-    returned = exchange(picked.reshape(devices, capacity, 16), ("gx", "gy"), False, 5)
+    returned = route_tiles(picked.reshape(devices, capacity, 16), (5, 7))
     own_vals = contract("ps,sk->pk", placing, returned.reshape(devices * capacity, 16))
     grad_widths = DELTA_EPS * jnp.sum(intersection * own_vals, axis=1)
     return (jnp.concatenate([e_steps[NT - 1], h_last]), focal_power, grad_widths)

time: 218 us -> 223 us (1.023)
  local copies, waits for them, and re-layouts: 20.4 us -> 24.5 us
    pallas_call x0 -> x2, local copies, waits for them, and re-layouts: none -> 3.21 us  [exchange(): pl.pallas_call(kernel, out_shape=jax.ShapeDtypeStruct((count,) + tuple(pi...]
    pallas_call x6 -> x8, Pallas kernels: 98.3 us -> 98.9 us  [exchange(): pl.pallas_call(kernel, out_shape=jax.ShapeDtypeStruct((count,) + tuple(pi...]
where the time goes in v2:
time: 223 us; the launch traced here: 222 us
  Pallas kernels  163 us (73%)
  other arithmetic  24.8 us (11%)
  local copies, waits for them, and re-layouts  24.5 us (11%)
  matrix products  8.74 us (4%)
    pallas_call x8, Pallas kernels, exchange(): pl.pallas_call(kernel, out_shape=jax.ShapeDtypeStruct((count,) + tuple(pi...  98.9 us
    pallas_call x2, Pallas kernels, run_leaps(): pl.pallas_call(kernel, out_shape=(jax.ShapeDtypeStruct((NT, 3, size_x, si...  64.1 us
    dot_general x16, matrix products, contract(): jnp.einsum(pattern, first_op, second_op, precision=lax.Precision.HIGHEST)  7.24 us
    sub x1, other arithmetic, shards(): changes.append((after - before)[:, :, :, ZM - ZP:ZM])  6.48 us

profile of v2, /device:TPU:1, one launch (start us, length us, event | category | flops | bytes accessed | tf_op | source)
XLA Modules:
  0.0 222.3 jit_solution(5390648856566070177)
XLA Ops:
  5.8 12.0 %shard_map.94 = f32[16,8,2,18]{3,2,1,0:T(2,128)} custom-call(f32[16,8,2,18]{3,2,1,0:T(2,128)} %bitcast.211), custom_call_target="tpu_custom_call" | custom-call | tf_op jit(solution)/shard_map/pallas_call | solution.py:321
  17.8 1.6 copy.109
  19.4 8.8 %shard_map.95 = f32[8,16,2,18]{3,2,1,0:T(2,128)} custom-call(f32[8,16,2,18]{3,2,1,0:T(2,128)} %bitcast.212), custom_call_target="tpu_custom_call" | custom-call | tf_op jit(solution)/shard_map/pallas_call | solution.py:321
  29.3 1.0 slice_convert_fusion
  31.6 2.5 %fusion.155 = (f32[3,32,32,128]{3,2,1,0:T(8,128)S(1)}, f32[3,32,32,128]{3,2,1,0:T(8,128)S(1)}) fusion(f32[6,32,32,128]{3,2,1,0:T(8,128)} %param.7), kind=kLoop, calls=%fused_computation.222 | loop fusion | bytes 6291456 | tf_op jit(solution)/shard_map/slice | solution.py:397
  34.0 33.0 %shard_map.96 = (f32[4,3,32,32,128]{4,3,2,1,0:T(8,128)}, f32[3,32,32,128]{3,2,1,0:T(8,128)S(1)}) custom-call(f32[3,32,32,128]{3,2,1,0:T(8,128)S(1)} %get-tuple-element.26.refs_0_, f32[3,32,32,128]{3,2,1,0:T(8,128)S(1)} %get-tuple-element.25.refs_1_, f32[32,32,128]{2,1,0:T(8,128)S(1)} %add_divide_fusion.refs_2_.refs_0_), custom_call_target="tpu_custom_call" | custom-call | tf_op jit(solution)/shard_map/pallas_call | solution.py:238
  67.0 3.5 %slice_bitcast_fusion.6 = (f32[3,32,32,128]{3,2,1,0:T(8,128)S(1)}, f32[3,32,32,128]{3,2,1,0:T(8,128)S(1)}, f32[3,32,32,128]{3,2,1,0:T(8,128)S(1)}, f32[3,32,32,128]{3,2,1,0:T(8,128)S(1)}) fusion(f32[4,3,32,32,128]{4,3,2,1,0:T(8,128)} %get-tuple-element.6), kind=kLoop, calls=%fused_computation.9 | loop fusion | bytes 12582912 | tf_op jit(solution)/shard_map/squeeze | solution.py:403
  70.6 1.1 multiply_add_fusion
  71.7 2.2 %pad_maximum_fusion = f32[6,32,32,128]{3,2,1,0:T(8,128)} fusion(f32[3,32,32,128]{3,2,1,0:T(8,128)S(1)} %get-tuple-element.7, f32[3,32,32,128]{3,2,1,0:T(8,128)S(1)} %get-tuple-element.24), kind=kLoop, calls=%fused_computation.1 | loop fusion | flops 786432 | bytes 6291456 | tf_op jit(solution)/shard_map/concatenate | solution.py:485
  74.6 6.5 %fusion.152 = (f32[3,32,32,128]{3,2,1,0:T(8,128)S(1)}, f32[3,32,32,128]{3,2,1,0:T(8,128)}, f32[3,32,32,128]{3,2,1,0:T(8,128)}, f32[3,32,32,128]{3,2,1,0:T(8,128)}) fusion(f32[4,3,32,32,128]{4,3,2,1,0:T(8,128)} %get-tuple-element.6, f32[6,32,32,128]{3,2,1,0:T(8,128)} %param.7), kind=kLoop, calls=%fused_computation.218 | loop fusion | flops 1572864 | bytes 14155776 | tf_op jit(solution)/shard_map/sub | solution.py:407
  83.9 1.1 reshape.171.x_ref
  84.9 10.1 %shard_map.97 = f32[8,32,128]{2,1,0:T(8,128)} custom-call(f32[8,32,128]{2,1,0:T(8,128)} %reshape.171.x_ref), custom_call_target="tpu_custom_call" | custom-call | tf_op jit(solution)/shard_map/pallas_call | solution.py:321
  98.7 21.6 %shard_map.98 = f32[16,8,256]{2,1,0:T(8,128)} custom-call(f32[16,8,256]{2,1,0:T(8,128)} %reshape.173.x_ref), custom_call_target="tpu_custom_call" | custom-call | tf_op jit(solution)/shard_map/pallas_call | solution.py:321
  122.6 9.4 %shard_map.99 = f32[16,8,256]{2,1,0:T(8,128)} custom-call(f32[8,256]{1,0:T(8,128)} %reshape.174.x_ref), custom_call_target="tpu_custom_call" | custom-call | tf_op jit(solution)/shard_map/pallas_call | solution.py:321
  135.5 6.7 %shard_map.100 = f32[8,32,128]{2,1,0:T(8,128)} custom-call(f32[32,128]{1,0:T(8,128)} %reshape.177.x_ref), custom_call_target="tpu_custom_call" | custom-call | tf_op jit(solution)/shard_map/pallas_call | solution.py:321
  142.2 1.3 reshape.192
  145.7 2.7 %broadcast_select_fusion.refs_1_ = f32[4,2,32,32,128]{4,3,2,1,0:T(8,128)} fusion(f32[4,2,32,32]{3,2,1,0:T(8,128)S(1)} %copy.80, pred[128]{0:T(512)(128)(4,1)S(1)} %iota_compare_fusion.8), kind=kLoop, calls=%fused_computation.2 | loop fusion | flops 1048576 | bytes 4227200 | tf_op jit(solution)/shard_map/jit(_where)/select_n | solution.py:470
  148.4 31.1 %shard_map.101 = (f32[4,3,32,32,128]{4,3,2,1,0:T(8,128)}, f32[3,32,32,128]{3,2,1,0:T(8,128)}) custom-call(f32[32,32,128]{2,1,0:T(8,128)S(1)} %add_divide_fusion.refs_2_.refs_0_, f32[4,2,32,32,128]{4,3,2,1,0:T(8,128)} %broadcast_select_fusion.refs_1_), custom_call_target="tpu_custom_call" | custom-call | tf_op jit(solution)/shard_map/pallas_call | solution.py:238
  179.5 3.7 %slice_bitcast_fusion.3 = (f32[3,32,32,128]{3,2,1,0:T(8,128)S(1)}, f32[3,32,32,128]{3,2,1,0:T(8,128)S(1)}, f32[3,32,32,128]{3,2,1,0:T(8,128)S(1)}, f32[3,32,32,128]{3,2,1,0:T(8,128)S(1)}) fusion(f32[4,3,32,32,128]{4,3,2,1,0:T(8,128)} %get-tuple-element.8), kind=kLoop, calls=%fused_computation.6 | loop fusion | bytes 12582912 | tf_op jit(solution)/shard_map/squeeze | solution.py:476
  183.7 3.6 %fusion.10 = f32[32,32]{1,0:T(8,128)S(1)} fusion(f32[3,32,32,128]{3,2,1,0:T(8,128)S(1)} %copy-done.3, f32[3,32,32,128]{3,2,1,0:T(8,128)S(1)} %get-tuple-element.12, f32[3,32,32,128]{3,2,1,0:T(8,128)S(1)} %copy-done.2, f32[3,32,32,128]{3,2,1,0:T(8,128)S(1)} %get-tuple-element.13, f32[3,32,32,128]{3,2,1,0:T(8,128)S(1)} %copy-done.1, ...), kind=kLoop, calls=%fused_computation.32 | loop fusion | flops 117760 | bytes 413696 | tf_op jit(solution)/shard_map/reduce_sum | solution.py:479
  188.7 21.8 %shard_map.102 = f32[16,8,2,16]{3,2,1,0:T(2,128)} custom-call(f32[16,8,2,16]{3,2,1,0:T(2,128)} %bitcast.214), custom_call_target="tpu_custom_call" | custom-call | tf_op jit(solution)/shard_map/pallas_call | solution.py:321
  210.6 1.6 copy.107
  212.2 8.3 %shard_map.103 = f32[8,16,2,16]{3,2,1,0:T(2,128)} custom-call(f32[8,16,2,16]{3,2,1,0:T(2,128)} %bitcast.215), custom_call_target="tpu_custom_call" | custom-call | tf_op jit(solution)/shard_map/pallas_call | solution.py:321
  220.5 1.2 fusion.5
  (87 shorter events, 24.3 us)
Async XLA Ops:
  0.6 1.0 copy-start
  3.2 28.1 %copy-start.4 = (f32[32,32,128]{2,1,0:T(8,128)S(1)}, f32[32,32,128]{2,1,0:T(8,128)}, u32[]{:S(2)}) copy-start(f32[32,32,128]{2,1,0:T(8,128)} %param.8) | copy-start | bytes 1572868
  179.5 3.8 %copy-start.1 = (f32[3,32,32,128]{3,2,1,0:T(8,128)S(1)}, f32[3,32,32,128]{3,2,1,0:T(8,128)}, u32[]{:S(2)}) copy-start(f32[3,32,32,128]{3,2,1,0:T(8,128)} %get-tuple-element.16) | copy-start | bytes 4718596
  179.5 3.8 %copy-start.2 = (f32[3,32,32,128]{3,2,1,0:T(8,128)S(1)}, f32[3,32,32,128]{3,2,1,0:T(8,128)}, u32[]{:S(2)}) copy-start(f32[3,32,32,128]{3,2,1,0:T(8,128)} %get-tuple-element.17) | copy-start | bytes 4718596
  179.5 4.2 %copy-start.3 = (f32[3,32,32,128]{3,2,1,0:T(8,128)S(1)}, f32[3,32,32,128]{3,2,1,0:T(8,128)}, u32[]{:S(2)}) copy-start(f32[3,32,32,128]{3,2,1,0:T(8,128)} %get-tuple-element.18) | copy-start | bytes 4718596
  187.3 33.2 %copy-start.5 = (f32[128,16]{0,1:T(8,128)S(1)}, f32[128,16]{0,1:T(8,128)}, u32[]{:S(2)}) copy-start(f32[128,16]{0,1:T(8,128)} %param.11) | copy-start | bytes 24580

commit v3 on v1

--- a/solution.py
+++ b/solution.py
@@ -328,6 +328,79 @@
     )(pieces)
 
 
+def focal_rows(pieces, weights, norm_scale, tag):
+    count, sizes = group_of(("gy",))
+    rows, width = pieces.shape[1:]
+
+    def kernel(x_ref, t_ref, far_ref, o_ref, got, held, send_sem, recv_sem):
+        me = lax.axis_index("gy")
+        barrier = pltpu.get_barrier_semaphore()
+        for step in range(1, count):
+            pl.semaphore_signal(
+                barrier, 1, device_id=(lax.axis_index("gx"), lax.rem(me + step, count)),
+                device_id_type=pl.DeviceIdType.MESH,
+            )
+        pl.semaphore_wait(barrier, count - 1)
+
+        def spread(phase, source_of):
+            copies = []
+            for step in range(1, count):
+                peer = lax.rem(me + step, count)
+                copy = pltpu.make_async_remote_copy(
+                    src_ref=source_of(peer),
+                    dst_ref=(got if phase == 0 else o_ref).at[me],
+                    send_sem=send_sem.at[phase * count + step],
+                    recv_sem=recv_sem.at[phase * count + step],
+                    device_id=(lax.axis_index("gx"), peer),
+                    device_id_type=pl.DeviceIdType.MESH,
+                )
+                copy.start()
+                copies.append(copy)
+            for copy in copies:
+                copy.wait_send()
+            for step in range(1, count):
+                source = lax.rem(me + count - step, count)
+                pltpu.make_async_remote_copy(
+                    src_ref=source_of(source),
+                    dst_ref=(got if phase == 0 else o_ref).at[source],
+                    send_sem=send_sem.at[phase * count + step],
+                    recv_sem=recv_sem.at[phase * count + step],
+                    device_id=(lax.axis_index("gx"), source),
+                    device_id_type=pl.DeviceIdType.MESH,
+                ).wait_recv()
+
+        got[me] = x_ref[me]
+        spread(0, lambda peer: x_ref.at[peer])
+        total = got[0]
+        for source in range(1, count):
+            total = total + got[source]
+        far = norm_scale * total
+        far_ref[...] = far
+        odd = lax.broadcasted_iota(jnp.int32, far.shape, 0) % 2 == 1
+        scaled = t_ref[...] * far
+        weighted = jnp.where(odd, -scaled, scaled)
+        held[...] = weighted
+        o_ref[me] = weighted
+        spread(1, lambda peer: held)
+
+    return pl.pallas_call(
+        kernel,
+        out_shape=(
+            jax.ShapeDtypeStruct((rows, width), jnp.float32),
+            jax.ShapeDtypeStruct((count, rows, width), jnp.float32),
+        ),
+        in_specs=[pl.BlockSpec(memory_space=pltpu.VMEM)] * 2,
+        out_specs=(pl.BlockSpec(memory_space=pltpu.VMEM),) * 2,
+        scratch_shapes=[
+            pltpu.VMEM((count, rows, width), jnp.float32),
+            pltpu.VMEM((rows, width), jnp.float32),
+            pltpu.SemaphoreType.DMA((2 * count,)),
+            pltpu.SemaphoreType.DMA((2 * count,)),
+        ],
+        compiler_params=pltpu.CompilerParams(collective_id=tag, has_side_effects=True),
+    )(pieces, weights)
+
+
 def kernel_table(count_out, count_in, offset, length):
     focal_pos = (jnp.arange(count_out, dtype=jnp.float32) + 0.5) / count_out - 0.5
     cell_pos = (
@@ -419,14 +492,16 @@
     )
     row_count = U // devices
     far = far.reshape(2, span_y, row_count, 2, V).transpose(1, 0, 2, 3, 4)
-    far = exchange(far.reshape(span_y, 2 * row_count * 2, V), ("gy",), False, 2)
-    far = norm_scale * jnp.sum(far, axis=0).reshape(2, row_count, 2, V)
+    mine_target = lax.dynamic_slice_in_dim(target, linear * row_count, row_count, 0)
+    row_weights = jnp.broadcast_to(mine_target[None, :, None, :], (2, row_count, 2, V))
+    far, weighted = focal_rows(
+        far.reshape(span_y, 2 * row_count * 2, V),
+        row_weights.reshape(2 * row_count * 2, V),
+        norm_scale,
+        2,
+    )
+    far = far.reshape(2, row_count, 2, V)
     focal_power = jnp.sum(far * far, axis=(0, 2))
-    mine_target = lax.dynamic_slice_in_dim(target, linear * row_count, row_count, 0)
-    weighted = jnp.stack(
-        [mine_target * far[:, :, 0], -(mine_target * far[:, :, 1])], axis=2
-    )
-    weighted = exchange(weighted.reshape(2 * row_count * 2, V), ("gy",), True, 3)
     weighted = weighted.reshape(span_y, 2, row_count, 2, V).transpose(1, 0, 2, 3, 4)
     weighted = weighted.reshape(2, span_y * row_count, 2, V)
     w_re, w_im = weighted[:, :, 0], weighted[:, :, 1]

time: 218 us -> 213 us (0.977)
  Pallas kernels: 161 us -> 157 us
    pallas_call x6 -> x4, Pallas kernels: 98.3 us -> 66.4 us  [exchange(): pl.pallas_call(kernel, out_shape=jax.ShapeDtypeStruct((count,) + tuple(pi...]
    pallas_call x0 -> x1, Pallas kernels: none -> 28.8 us  [focal_rows(): pl.pallas_call(kernel, out_shape=(jax.ShapeDtypeStruct((rows, width), jnp...]
where the time goes in v3:
time: 213 us; the launch traced here: 212 us
  Pallas kernels  157 us (74%)
  other arithmetic  24.6 us (12%)
  local copies, waits for them, and re-layouts  20.4 us (10%)
  matrix products  9.4 us (4%)
    pallas_call x4, Pallas kernels, exchange(): pl.pallas_call(kernel, out_shape=jax.ShapeDtypeStruct((count,) + tuple(pi...  66.4 us
    pallas_call x2, Pallas kernels, run_leaps(): pl.pallas_call(kernel, out_shape=(jax.ShapeDtypeStruct((NT, 3, size_x, si...  61.5 us
    pallas_call x1, Pallas kernels, focal_rows(): pl.pallas_call(kernel, out_shape=(jax.ShapeDtypeStruct((rows, width), jnp...  28.8 us
    dot_general x16, matrix products, contract(): jnp.einsum(pattern, first_op, second_op, precision=lax.Precision.HIGHEST)  7.9 us
    sub x1, other arithmetic, shards(): changes.append((after - before)[:, :, :, ZM - ZP:ZM])  6.48 us

profile of v3, /device:TPU:1, one launch (start us, length us, event | category | flops | bytes accessed | tf_op | source)
XLA Modules:
  0.0 212.3 jit_solution(4083377727170068322)
XLA Ops:
  5.3 1.0 fusion.34
  6.3 20.7 %shard_map.94 = f32[128,2,18]{2,1,0:T(2,128)} custom-call(f32[128,2,18]{2,1,0:T(2,128)} %bitcast.197), custom_call_target="tpu_custom_call" | custom-call | tf_op jit(solution)/shard_map/pallas_call | solution.py:321
  27.1 1.0 mul.233
  28.1 1.0 slice_convert_fusion
  30.3 2.5 %fusion.154 = (f32[3,32,32,128]{3,2,1,0:T(8,128)S(1)}, f32[3,32,32,128]{3,2,1,0:T(8,128)S(1)}) fusion(f32[6,32,32,128]{3,2,1,0:T(8,128)} %param.7), kind=kLoop, calls=%fused_computation.212 | loop fusion | bytes 6291456 | tf_op jit(solution)/shard_map/slice | solution.py:460
  32.8 31.9 %shard_map.95 = (f32[4,3,32,32,128]{4,3,2,1,0:T(8,128)}, f32[3,32,32,128]{3,2,1,0:T(8,128)S(1)}) custom-call(f32[3,32,32,128]{3,2,1,0:T(8,128)S(1)} %get-tuple-element.30.refs_0_, f32[3,32,32,128]{3,2,1,0:T(8,128)S(1)} %get-tuple-element.29.refs_1_, f32[32,32,128]{2,1,0:T(8,128)S(1)} %add_divide_fusion.refs_2_.refs_0_), custom_call_target="tpu_custom_call" | custom-call | tf_op jit(solution)/shard_map/pallas_call | solution.py:238
  64.7 3.5 %slice_bitcast_fusion.6 = (f32[3,32,32,128]{3,2,1,0:T(8,128)S(1)}, f32[3,32,32,128]{3,2,1,0:T(8,128)S(1)}, f32[3,32,32,128]{3,2,1,0:T(8,128)S(1)}, f32[3,32,32,128]{3,2,1,0:T(8,128)S(1)}) fusion(f32[4,3,32,32,128]{4,3,2,1,0:T(8,128)} %get-tuple-element.8), kind=kLoop, calls=%fused_computation.9 | loop fusion | bytes 12582912 | tf_op jit(solution)/shard_map/squeeze | solution.py:466
  68.3 1.1 multiply_add_fusion
  69.4 2.2 %pad_maximum_fusion = f32[6,32,32,128]{3,2,1,0:T(8,128)} fusion(f32[3,32,32,128]{3,2,1,0:T(8,128)S(1)} %get-tuple-element.9, f32[3,32,32,128]{3,2,1,0:T(8,128)S(1)} %get-tuple-element.28), kind=kLoop, calls=%fused_computation.1 | loop fusion | flops 786432 | bytes 6291456 | tf_op jit(solution)/shard_map/concatenate | solution.py:550
  72.3 6.5 %fusion.151 = (f32[3,32,32,128]{3,2,1,0:T(8,128)S(1)}, f32[3,32,32,128]{3,2,1,0:T(8,128)}, f32[3,32,32,128]{3,2,1,0:T(8,128)}, f32[3,32,32,128]{3,2,1,0:T(8,128)}) fusion(f32[4,3,32,32,128]{4,3,2,1,0:T(8,128)} %get-tuple-element.8, f32[6,32,32,128]{3,2,1,0:T(8,128)} %param.7), kind=kLoop, calls=%fused_computation.208 | loop fusion | flops 1572864 | bytes 14155776 | tf_op jit(solution)/shard_map/sub | solution.py:470
  81.5 1.1 reshape.181.x_ref
  82.6 9.3 %shard_map.96 = f32[8,32,128]{2,1,0:T(8,128)} custom-call(f32[8,32,128]{2,1,0:T(8,128)} %reshape.181.x_ref), custom_call_target="tpu_custom_call" | custom-call | tf_op jit(solution)/shard_map/pallas_call | solution.py:321
  91.9 0.9 reduce_sum.58
  95.7 28.8 %shard_map.97 = (f32[8,256]{1,0:T(8,128)}, f32[16,8,256]{2,1,0:T(8,128)}) custom-call(f32[16,8,256]{2,1,0:T(8,128)} %reshape.183.x_ref, f32[8,256]{1,0:T(8,128)} %reshape.184.t_ref), custom_call_target="tpu_custom_call" | custom-call | tf_op jit(solution)/shard_map/pallas_call | solution.py:386
  125.8 1.0 reshape.185
  129.3 6.7 %shard_map.98 = f32[8,32,128]{2,1,0:T(8,128)} custom-call(f32[32,128]{1,0:T(8,128)} %reshape.187.x_ref), custom_call_target="tpu_custom_call" | custom-call | tf_op jit(solution)/shard_map/pallas_call | solution.py:321
  136.0 1.3 reshape.203
  139.5 2.7 %broadcast_select_fusion.refs_1_ = f32[4,2,32,32,128]{4,3,2,1,0:T(8,128)} fusion(f32[4,2,32,32]{3,2,1,0:T(8,128)S(1)} %copy.69, pred[128]{0:T(512)(128)(4,1)S(1)} %iota_compare_fusion.8), kind=kLoop, calls=%fused_computation.2 | loop fusion | flops 1048576 | bytes 4227200 | tf_op jit(solution)/shard_map/jit(_where)/select_n | solution.py:535
  142.2 29.6 %shard_map.99 = (f32[4,3,32,32,128]{4,3,2,1,0:T(8,128)}, f32[3,32,32,128]{3,2,1,0:T(8,128)}) custom-call(f32[32,32,128]{2,1,0:T(8,128)S(1)} %add_divide_fusion.refs_2_.refs_0_, f32[4,2,32,32,128]{4,3,2,1,0:T(8,128)} %broadcast_select_fusion.refs_1_), custom_call_target="tpu_custom_call" | custom-call | tf_op jit(solution)/shard_map/pallas_call | solution.py:238
  171.8 3.7 %slice_bitcast_fusion.3 = (f32[3,32,32,128]{3,2,1,0:T(8,128)S(1)}, f32[3,32,32,128]{3,2,1,0:T(8,128)S(1)}, f32[3,32,32,128]{3,2,1,0:T(8,128)S(1)}, f32[3,32,32,128]{3,2,1,0:T(8,128)S(1)}) fusion(f32[4,3,32,32,128]{4,3,2,1,0:T(8,128)} %get-tuple-element.12), kind=kLoop, calls=%fused_computation.6 | loop fusion | bytes 12582912 | tf_op jit(solution)/shard_map/squeeze | solution.py:541
  176.0 3.6 %fusion.10 = f32[32,32]{1,0:T(8,128)S(1)} fusion(f32[3,32,32,128]{3,2,1,0:T(8,128)S(1)} %copy-done.3, f32[3,32,32,128]{3,2,1,0:T(8,128)S(1)} %get-tuple-element.16, f32[3,32,32,128]{3,2,1,0:T(8,128)S(1)} %copy-done.2, f32[3,32,32,128]{3,2,1,0:T(8,128)S(1)} %get-tuple-element.17, f32[3,32,32,128]{3,2,1,0:T(8,128)S(1)} %copy-done.1, ...), kind=kLoop, calls=%fused_computation.32 | loop fusion | flops 117760 | bytes 413696 | tf_op jit(solution)/shard_map/reduce_sum | solution.py:544
  180.1 0.9 reshape_reshape.3.x_ref
  180.9 29.6 %shard_map.100 = f32[128,2,16]{2,1,0:T(2,128)} custom-call(f32[128,2,16]{2,1,0:T(2,128)} %reshape_reshape.3.x_ref), custom_call_target="tpu_custom_call" | custom-call | tf_op jit(solution)/shard_map/pallas_call | solution.py:321
  210.6 1.2 fusion.5
  (78 shorter events, 19.3 us)
Async XLA Ops:
  0.6 1.0 copy-start
  0.6 29.5 %copy-start.4 = (f32[32,32,128]{2,1,0:T(8,128)S(1)}, f32[32,32,128]{2,1,0:T(8,128)}, u32[]{:S(2)}) copy-start(f32[32,32,128]{2,1,0:T(8,128)} %param.8) | copy-start | bytes 1572868
  171.8 3.8 %copy-start.1 = (f32[3,32,32,128]{3,2,1,0:T(8,128)S(1)}, f32[3,32,32,128]{3,2,1,0:T(8,128)}, u32[]{:S(2)}) copy-start(f32[3,32,32,128]{3,2,1,0:T(8,128)} %get-tuple-element.20) | copy-start | bytes 4718596
  171.8 3.8 %copy-start.2 = (f32[3,32,32,128]{3,2,1,0:T(8,128)S(1)}, f32[3,32,32,128]{3,2,1,0:T(8,128)}, u32[]{:S(2)}) copy-start(f32[3,32,32,128]{3,2,1,0:T(8,128)} %get-tuple-element.21) | copy-start | bytes 4718596
  171.8 4.2 %copy-start.3 = (f32[3,32,32,128]{3,2,1,0:T(8,128)S(1)}, f32[3,32,32,128]{3,2,1,0:T(8,128)}, u32[]{:S(2)}) copy-start(f32[3,32,32,128]{3,2,1,0:T(8,128)} %get-tuple-element.22) | copy-start | bytes 4718596
  176.0 34.6 %copy-start.5 = (f32[128,16]{0,1:T(8,128)S(1)}, f32[128,16]{0,1:T(8,128)}, u32[]{:S(2)}) copy-start(f32[128,16]{0,1:T(8,128)} %param.11) | copy-start | bytes 24580

commit v4 on v3

--- a/solution.py
+++ b/solution.py
@@ -59,23 +59,23 @@
     return (elec_x, elec_y, elec_z, magn_x, magn_y, magn_z)
 
 
-def run_leaps(e_start, h_start, inv_eps, drive, tag):
+def run_leaps(fields, inv_eps, history, drive, tag):
     span_x = lax.axis_size("gx")
     span_y = lax.axis_size("gy")
     size_x, size_y, size_z = inv_eps.shape
-    zero_start = e_start is None
-    with_drive = drive is not None
+    adjoint = history is not None
     mesh_id = pl.DeviceIdType.MESH
 
     def kernel(*refs):
         refs = list(refs)
-        if zero_start:
-            e_in = h_in = None
+        if adjoint:
+            f_in, hist, eps_ref, drv, acc = refs[:5]
+            a_hist, h_state = refs[5:7]
+            rest = refs[7:]
         else:
-            e_in, h_in = refs.pop(0), refs.pop(0)
-        eps_ref = refs.pop(0)
-        drv = refs.pop(0) if with_drive else None
-        e_out, h_out, east, north, west, south, xs_e, ys_e, xs_h, ys_h, ssem, rsem = refs
+            f_in, eps_ref, final, e_hist = refs[:4]
+            rest = refs[4:]
+        east, north, west, south, xs_e, ys_e, xs_h, ys_h, ssem, rsem = rest
         px = lax.axis_index("gx")
         py = lax.axis_index("gy")
         barrier = pltpu.get_barrier_semaphore()
@@ -109,13 +109,32 @@
 
         def load_e(step, comp, x):
             if step == 0:
-                return zero_slab if zero_start else e_in[comp, x]
-            return e_out[step - 1, comp, x]
+                return zero_slab if adjoint else f_in[comp, x]
+            if adjoint:
+                return a_hist[(step - 1) % 2, comp, x]
+            return e_hist[step - 1, comp, x]
+
+        def store_e(step, comp, x, value):
+            if adjoint:
+                a_hist[step % 2, comp, x] = value
+            else:
+                e_hist[step, comp, x] = value
+                if step == NT - 1:
+                    final[comp, x] = value
 
         def load_h(step, comp, x):
             if step == 0:
-                return zero_slab if zero_start else h_in[comp, x]
-            return h_out[comp, x]
+                return zero_slab if adjoint else f_in[3 + comp, x]
+            return h_state[comp, x] if adjoint else final[3 + comp, x]
+
+        def store_h(comp, x, value):
+            if adjoint:
+                h_state[comp, x] = value
+            else:
+                final[3 + comp, x] = value
+
+        def forward_e(n, comp, x):
+            return f_in[comp, x] if n == 0 else hist[n - 1, comp, x]
 
         def swap(src_x, dst_x, src_y, dst_y, sem, to_x, to_y, sends_x, sends_y, gets_x, gets_y):
             copy_x = pltpu.make_async_remote_copy(
@@ -142,19 +161,19 @@
             pl.when(sends_x)(copy_x.wait_send)
             pl.when(sends_y)(copy_y.wait_send)
 
-        if not zero_start:
-            xs_e[0, 0] = e_in[1, 0]
-            xs_e[0, 1] = e_in[2, 0]
+        if not adjoint:
+            xs_e[0, 0] = f_in[1, 0]
+            xs_e[0, 1] = f_in[2, 0]
 
             def stage_first(x, carry):
-                ys_e[0, 0, pl.ds(x, 1), :] = e_in[0, x][0:1, :]
-                ys_e[0, 1, pl.ds(x, 1), :] = e_in[2, x][0:1, :]
+                ys_e[0, 0, pl.ds(x, 1), :] = f_in[0, x][0:1, :]
+                ys_e[0, 1, pl.ds(x, 1), :] = f_in[2, x][0:1, :]
                 return carry
 
             lax.fori_loop(0, size_x, stage_first, 0)
 
         for step in range(NT):
-            if step == 0 and zero_start:
+            if step == 0 and adjoint:
                 east[0] = jnp.zeros(east.shape[1:], jnp.float32)
                 north[0] = jnp.zeros(north.shape[1:], jnp.float32)
             else:
@@ -176,9 +195,9 @@
                 hx = load_h(step, 0, x) - COURANT * curl_x
                 hy = load_h(step, 1, x) - COURANT * curl_y
                 hz = load_h(step, 2, x) - COURANT * curl_z
-                h_out[0, x] = hx
-                h_out[1, x] = hy
-                h_out[2, x] = hz
+                store_h(0, x, hx)
+                store_h(1, x, hy)
+                store_h(2, x, hz)
                 ys_h[step, 0, pl.ds(x, 1), :] = hx[size_y - 1 : size_y, :]
                 ys_h[step, 1, pl.ds(x, 1), :] = hz[size_y - 1 : size_y, :]
                 return hy, hz
@@ -198,24 +217,33 @@
             )
 
             def electric(x, hy_prev, hz_prev, step=step):
-                hx = h_out[0, x]
-                hy = h_out[1, x]
-                hz = h_out[2, x]
+                hx = load_h(step + 1, 0, x)
+                hy = load_h(step + 1, 1, x)
+                hz = load_h(step + 1, 2, x)
                 sx_row = south[step, 0, pl.ds(x, 1), :]
                 sz_row = south[step, 1, pl.ds(x, 1), :]
                 curl_x = (hz - down_y(hz, sz_row)) - (hy - down_z(hy))
                 curl_y = (hx - down_z(hx)) - (hz - hz_prev)
                 curl_z = (hy - hy_prev) - (hx - down_y(hx, sx_row))
-                if with_drive:
+                if adjoint:
                     curl_x = curl_x - drv[step, 0, x]
                     curl_y = curl_y - drv[step, 1, x]
                 scale = eps_ref[x]
                 ex = load_e(step, 0, x) + COURANT * curl_x * scale
                 ey = load_e(step, 1, x) + COURANT * curl_y * scale
                 ez = load_e(step, 2, x) + COURANT * curl_z * scale
-                e_out[step, 0, x] = ex
-                e_out[step, 1, x] = ey
-                e_out[step, 2, x] = ez
+                store_e(step, 0, x, ex)
+                store_e(step, 1, x, ey)
+                store_e(step, 2, x, ez)
+                if adjoint:
+                    moment = NT - step
+                    product = (
+                        ex * (forward_e(moment, 0, x) - forward_e(moment - 1, 0, x))
+                        + ey * (forward_e(moment, 1, x) - forward_e(moment - 1, 1, x))
+                        + ez * (forward_e(moment, 2, x) - forward_e(moment - 1, 2, x))
+                    )
+                    before = zero_slab if step == 0 else acc[x]
+                    acc[x] = before - product * scale
                 if step + 1 < NT:
                     ys_e[step + 1, 0, pl.ds(x, 1), :] = ex[0:1, :]
                     ys_e[step + 1, 1, pl.ds(x, 1), :] = ez[0:1, :]
@@ -227,29 +255,42 @@
                 xs_e[step + 1, 1] = ez_first
 
             def electric_body(x, carry, step=step):
-                electric(x, h_out[1, x - 1], h_out[2, x - 1])
+                electric(x, load_h(step + 1, 1, x - 1), load_h(step + 1, 2, x - 1))
                 return carry
 
             lax.fori_loop(1, size_x, electric_body, 0, unroll=True)
 
     rim_x = pltpu.VMEM((NT, 2, size_y, size_z), jnp.float32)
     rim_y = pltpu.VMEM((NT, 2, size_x, size_z), jnp.float32)
-    operands = ([] if zero_start else [e_start, h_start]) + [inv_eps] + ([drive] if with_drive else [])
+    field_shape = (size_x, size_y, size_z)
+    if adjoint:
+        operands = [fields, history, inv_eps, drive]
+        out_shape = jax.ShapeDtypeStruct(field_shape, jnp.float32)
+        out_specs = pl.BlockSpec(memory_space=pltpu.VMEM)
+        state = [
+            pltpu.VMEM((2, 3) + field_shape, jnp.float32),
+            pltpu.VMEM((3,) + field_shape, jnp.float32),
+        ]
+    else:
+        operands = [fields, inv_eps]
+        out_shape = (
+            jax.ShapeDtypeStruct((6,) + field_shape, jnp.float32),
+            jax.ShapeDtypeStruct((NT, 3) + field_shape, jnp.float32),
+        )
+        out_specs = (pl.BlockSpec(memory_space=pltpu.VMEM),) * 2
+        state = []
     return pl.pallas_call(
         kernel,
-        out_shape=(
-            jax.ShapeDtypeStruct((NT, 3, size_x, size_y, size_z), jnp.float32),
-            jax.ShapeDtypeStruct((3, size_x, size_y, size_z), jnp.float32),
-        ),
+        out_shape=out_shape,
         in_specs=[pl.BlockSpec(memory_space=pltpu.VMEM)] * len(operands),
-        out_specs=(pl.BlockSpec(memory_space=pltpu.VMEM),) * 2,
-        scratch_shapes=[
+        out_specs=out_specs,
+        scratch_shapes=state + [
             rim_x, rim_y, rim_x, rim_y, rim_x, rim_y, rim_x, rim_y,
             pltpu.SemaphoreType.DMA((4 * NT,)),
             pltpu.SemaphoreType.DMA((4 * NT,)),
         ],
         compiler_params=pltpu.CompilerParams(
-            collective_id=tag, has_side_effects=True, vmem_limit_bytes=48 * 1024 * 1024
+            collective_id=tag, has_side_effects=True, vmem_limit_bytes=56 * 1024 * 1024
         ),
     )(*operands)
 
@@ -456,19 +497,13 @@
     layers = ((z_index >= ZM - ZP) & (z_index < ZM)).astype(jnp.float32)
     permittivity = eps_background + DELTA_EPS * filling[:, :, None] * layers[None, None, :]
     inv_eps = 1.0 / permittivity
-    fields_now = tuple((fields[component] for component in range(6)))
-    e_steps, h_last = run_leaps(fields[:3], fields[3:], inv_eps, None, 10)
+    final_fields, e_steps = run_leaps(fields, inv_eps, None, None, 10)
     mon_re = jnp.zeros((2, TILE, TILE), jnp.float32)
     mon_im = jnp.zeros((2, TILE, TILE), jnp.float32)
-    changes = []
-    before = fields[:3]
     for moment in range(1, NT + 1):
-        after = e_steps[moment - 1]
-        monitor = after[0:2, :, :, ZM]
+        monitor = e_steps[moment - 1, 0:2, :, :, ZM]
         mon_re = mon_re + math.cos(ANGULAR_STEP * moment) * monitor
         mon_im = mon_im - math.sin(ANGULAR_STEP * moment) * monitor
-        changes.append((after - before)[:, :, :, ZM - ZP : ZM])
-        before = after
     norm_scale = (TILE * span_x * TILE * span_y) ** (-0.5)
     x_re, x_im = kernel_table(U, TILE * span_x, place_x * TILE, TILE)
     y_re, y_im = kernel_table(V, TILE * span_y, place_y * TILE, TILE)
@@ -521,7 +556,6 @@
     back_im = 2.0 * norm_scale * (
         contract("ux,cuy->cxy", x_re, half_im) + contract("ux,cuy->cxy", x_im, half_re)
     )
-    inv_layer = inv_eps[:, :, ZM - ZP : ZM]
     drives = []
     for moment in range(1, NT + 1):
         source_step = NT + 1 - moment
@@ -533,21 +567,14 @@
     drive = jnp.stack(drives)
     z_index = jnp.arange(fields.shape[3], dtype=jnp.int32)
     drive = jnp.where(z_index == ZM, drive[..., None], 0.0)
-    a_steps, _ = run_leaps(None, None, inv_eps, drive, 11)
-    grad_eps = jnp.zeros((TILE, TILE, ZP), jnp.float32)
-    for moment in range(1, NT + 1):
-        source_step = NT + 1 - moment
-        change = changes[source_step - 1]
-        adjoint = a_steps[moment - 1][:, :, :, ZM - ZP : ZM]
-        product = adjoint[0] * change[0] + adjoint[1] * change[1] + adjoint[2] * change[2]
-        grad_eps = grad_eps - product * inv_layer
-    column_grad = jnp.sum(grad_eps, axis=2)
+    grad_eps = run_leaps(fields, inv_eps, e_steps, drive, 11)
+    column_grad = jnp.sum(grad_eps[:, :, ZM - ZP : ZM], axis=2)
     spread = contract("sx,xy->sy", pick_x, column_grad)
     picked = jnp.sum(spread * pick_y, axis=1).reshape(devices * capacity, 16)
     returned = exchange(picked.reshape(devices, capacity, 16), ("gx", "gy"), False, 5)
     own_vals = contract("ps,sk->pk", placing, returned.reshape(devices * capacity, 16))
     grad_widths = DELTA_EPS * jnp.sum(intersection * own_vals, axis=1)
-    return (jnp.concatenate([e_steps[NT - 1], h_last]), focal_power, grad_widths)
+    return (final_fields, focal_power, grad_widths)
 
 
 def solution(mesh):

time: 213 us -> 202 us (0.948)
  local copies, waits for them, and re-layouts: 20.4 us -> 12 us
  other arithmetic: 24.6 us -> 17.7 us
  Pallas kernels: 157 us -> 161 us
    squeeze x2 -> x0, local copies, waits for them, and re-layouts: 7.28 us -> none  [the longest x1 3.73 us: shards(): adjoint = a_steps[moment - 1][:, :, :, ZM - ZP:ZM]]
    sub x1 -> x0, other arithmetic: 6.48 us -> none  [shards(): changes.append((after - before)[:, :, :, ZM - ZP:ZM])]
    pallas_call x2, Pallas kernels: 61.5 us -> 66.1 us  [run_leaps(): pl.pallas_call(kernel, out_shape=out_shape, in_specs=[pl.BlockSpec(memory...]
    slice x1 -> x0, local copies, waits for them, and re-layouts: 2.45 us -> none  [shards(): e_steps, h_last = run_leaps(fields[:3], fields[3:], inv_eps, None, 10)]
    concatenate x1 -> x0, other arithmetic: 2.25 us -> none  [shards(): jnp.concatenate([e_steps[NT - 1], h_last])]
    reduce_sum x1, other arithmetic: 3.59 us -> 1.42 us  [shards(): column_grad = jnp.sum(grad_eps[:, :, ZM - ZP:ZM], axis=2)]
    add x1, other arithmetic: 1.15 us -> 3.32 us  [shards(): mon_re = mon_re + math.cos(ANGULAR_STEP * moment) * monitor]
where the time goes in v4:
time: 202 us; the launch traced here: 201 us
  Pallas kernels  161 us (80%)
  other arithmetic  17.7 us (9%)
  local copies, waits for them, and re-layouts  12 us (6%)
  matrix products  9.18 us (5%)
    pallas_call x2, Pallas kernels, run_leaps(): pl.pallas_call(kernel, out_shape=out_shape, in_specs=[pl.BlockSpec(memory...  66.1 us
    pallas_call x4, Pallas kernels, exchange(): pl.pallas_call(kernel, out_shape=jax.ShapeDtypeStruct((count,) + tuple(pi...  66.1 us
    pallas_call x1, Pallas kernels, focal_rows(): pl.pallas_call(kernel, out_shape=(jax.ShapeDtypeStruct((rows, width), jnp...  28.9 us
    dot_general x16, matrix products, contract(): jnp.einsum(pattern, first_op, second_op, precision=lax.Precision.HIGHEST)  7.68 us

profile of v4, /device:TPU:1, one launch (start us, length us, event | category | flops | bytes accessed | tf_op | source)
XLA Modules:
  0.0 201.1 jit_solution(5969936761627119325)
XLA Ops:
  3.8 0.8 select_reduce_fusion
  5.3 1.0 fusion.13
  6.3 20.7 %shard_map.94 = f32[128,2,18]{2,1,0:T(2,128)} custom-call(f32[128,2,18]{2,1,0:T(2,128)} %bitcast.135), custom_call_target="tpu_custom_call" | custom-call | tf_op jit(solution)/shard_map/pallas_call | solution.py:362
  27.0 1.0 mul.173
  28.1 1.0 slice_convert_fusion
  30.1 2.0 %add_divide_fusion.refs_1_.refs_2_ = f32[32,32,128]{2,1,0:T(8,128)} fusion(f32[32,32,128]{2,1,0:T(8,128)} %param.8, f32[128]{0:T(128)S(1)} %and_convert_fusion, f32[32,32]{1,0:T(8,128)S(1)} %convolution_multiply_fusion), kind=kLoop, calls=%fused_computation.20 | loop fusion | flops 393216 | bytes 1053184 | tf_op jit(solution)/shard_map/div | solution.py:499
  32.2 34.7 %shard_map.95 = (f32[6,32,32,128]{3,2,1,0:T(8,128)}, f32[4,3,32,32,128]{4,3,2,1,0:T(8,128)}) custom-call(f32[6,32,32,128]{3,2,1,0:T(8,128)} %refs_0_.3, f32[32,32,128]{2,1,0:T(8,128)} %add_divide_fusion.refs_1_.refs_2_), custom_call_target="tpu_custom_call" | custom-call | tf_op jit(solution)/shard_map/pallas_call | solution.py:282
  66.8 3.3 %multiply_add_fusion = (f32[1,2,32,32,1]{4,3,2,1,0:T(8,128)S(1)}, f32[1,2,32,32,1]{4,3,2,1,0:T(8,128)S(1)}) fusion(f32[4,3,32,32,128]{4,3,2,1,0:T(8,128)} %get-tuple-element.8.refs_1_), kind=kLoop, calls=%fused_computation.17 | loop fusion | flops 30720 | bytes 49152 | tf_op jit(solution)/shard_map/add | solution.py:505
  73.6 1.1 reshape.161.x_ref
  74.6 9.2 %shard_map.96 = f32[8,32,128]{2,1,0:T(8,128)} custom-call(f32[8,32,128]{2,1,0:T(8,128)} %reshape.161.x_ref), custom_call_target="tpu_custom_call" | custom-call | tf_op jit(solution)/shard_map/pallas_call | solution.py:362
  83.8 0.9 reduce_sum.58
  86.8 0.7 reshape.163.x_ref
  87.6 28.9 %shard_map.97 = (f32[8,256]{1,0:T(8,128)}, f32[16,8,256]{2,1,0:T(8,128)}) custom-call(f32[16,8,256]{2,1,0:T(8,128)} %reshape.163.x_ref, f32[8,256]{1,0:T(8,128)} %reshape.164.t_ref), custom_call_target="tpu_custom_call" | custom-call | tf_op jit(solution)/shard_map/pallas_call | solution.py:427
  116.5 0.8 mul.196
  117.9 1.0 reshape.165
  121.3 6.7 %shard_map.98 = f32[8,32,128]{2,1,0:T(8,128)} custom-call(f32[32,128]{1,0:T(8,128)} %reshape.167.x_ref), custom_call_target="tpu_custom_call" | custom-call | tf_op jit(solution)/shard_map/pallas_call | solution.py:362
  128.0 1.3 reshape.183
  131.4 2.7 %broadcast_select_fusion.refs_3_ = f32[4,2,32,32,128]{4,3,2,1,0:T(8,128)} fusion(f32[4,2,32,32]{3,2,1,0:T(8,128)S(1)} %copy.69, pred[128]{0:T(512)(128)(4,1)S(1)} %iota_compare_fusion.8), kind=kLoop, calls=%fused_computation.1 | loop fusion | flops 1048576 | bytes 4227200 | tf_op jit(solution)/shard_map/jit(_where)/select_n | solution.py:569
  134.0 31.4 %shard_map.99 = f32[32,32,128]{2,1,0:T(8,128)} custom-call(f32[6,32,32,128]{3,2,1,0:T(8,128)} %refs_0_.3, f32[4,3,32,32,128]{4,3,2,1,0:T(8,128)} %get-tuple-element.8.refs_1_, f32[32,32,128]{2,1,0:T(8,128)} %add_divide_fusion.refs_1_.refs_2_, f32[4,2,32,32,128]{4,3,2,1,0:T(8,128)} %broadcast_select_fusion.refs_3_), custom_call_target="tpu_custom_call" | custom-call | tf_op jit(solution)/shard_map/pallas_call | solution.py:282
  165.5 1.4 slice_reduce_fusion
  167.4 0.9 reshape_reshape.3.x_ref
  168.2 29.5 %shard_map.100 = f32[128,2,16]{2,1,0:T(2,128)} custom-call(f32[128,2,16]{2,1,0:T(2,128)} %reshape_reshape.3.x_ref), custom_call_target="tpu_custom_call" | custom-call | tf_op jit(solution)/shard_map/pallas_call | solution.py:362
  197.7 1.2 fusion.5
  199.4 1.7 copy.90
  (68 shorter events, 16.1 us)
Async XLA Ops:
  0.6 1.0 copy-start
  134.0 63.7 %copy-start.2 = (f32[128,16]{0,1:T(8,128)S(1)}, f32[128,16]{0,1:T(8,128)}, u32[]{:S(2)}) copy-start(f32[128,16]{0,1:T(8,128)} %param.11) | copy-start | bytes 24580
  134.0 65.4 %copy-start.1 = (f32[6,32,32,128]{3,2,1,0:T(8,128)S(1)}, f32[6,32,32,128]{3,2,1,0:T(8,128)}, u32[]{:S(2)}) copy-start(f32[6,32,32,128]{3,2,1,0:T(8,128)} %get-tuple-element.26) | copy-start | bytes 9437188

commit v5 on v4

--- a/solution.py
+++ b/solution.py
@@ -123,8 +123,10 @@
                     final[comp, x] = value
 
         def load_h(step, comp, x):
+            if adjoint and step <= 1:
+                return zero_slab
             if step == 0:
-                return zero_slab if adjoint else f_in[3 + comp, x]
+                return f_in[3 + comp, x]
             return h_state[comp, x] if adjoint else final[3 + comp, x]
 
         def store_h(comp, x, value):
@@ -173,58 +175,63 @@
             lax.fori_loop(0, size_x, stage_first, 0)
 
         for step in range(NT):
-            if step == 0 and adjoint:
-                east[0] = jnp.zeros(east.shape[1:], jnp.float32)
-                north[0] = jnp.zeros(north.shape[1:], jnp.float32)
-            else:
+            if not (step == 0 and adjoint):
                 swap(
                     xs_e.at[step], east.at[step], ys_e.at[step], north.at[step], 4 * step,
                     lax.rem(px + span_x - 1, span_x), lax.rem(py + span_y - 1, span_y),
                     has_west, has_south, has_east, has_north,
                 )
 
-            def magnetic(x, ey_next, ez_next, step=step):
-                ex = load_e(step, 0, x)
-                ey = load_e(step, 1, x)
-                ez = load_e(step, 2, x)
-                nx_row = north[step, 0, pl.ds(x, 1), :]
-                nz_row = north[step, 1, pl.ds(x, 1), :]
-                curl_x = (up_y(ez, nz_row) - ez) - (up_z(ey) - ey)
-                curl_y = (up_z(ex) - ex) - (ez_next - ez)
-                curl_z = (ey_next - ey) - (up_y(ex, nx_row) - ex)
-                hx = load_h(step, 0, x) - COURANT * curl_x
-                hy = load_h(step, 1, x) - COURANT * curl_y
-                hz = load_h(step, 2, x) - COURANT * curl_z
-                store_h(0, x, hx)
-                store_h(1, x, hy)
-                store_h(2, x, hz)
-                ys_h[step, 0, pl.ds(x, 1), :] = hx[size_y - 1 : size_y, :]
-                ys_h[step, 1, pl.ds(x, 1), :] = hz[size_y - 1 : size_y, :]
-                return hy, hz
-
-            def magnetic_body(x, carry, step=step):
-                magnetic(x, load_e(step, 1, x + 1), load_e(step, 2, x + 1))
-                return carry
-
-            lax.fori_loop(0, size_x - 1, magnetic_body, 0, unroll=True)
-            hy_last, hz_last = magnetic(size_x - 1, east[step, 0], east[step, 1])
-            xs_h[step, 0] = hy_last
-            xs_h[step, 1] = hz_last
-            swap(
-                xs_h.at[step], west.at[step], ys_h.at[step], south.at[step], 4 * step + 2,
-                lax.rem(px + 1, span_x), lax.rem(py + 1, span_y),
-                has_east, has_north, has_west, has_south,
-            )
-
-            def electric(x, hy_prev, hz_prev, step=step):
-                hx = load_h(step + 1, 0, x)
-                hy = load_h(step + 1, 1, x)
-                hz = load_h(step + 1, 2, x)
-                sx_row = south[step, 0, pl.ds(x, 1), :]
-                sz_row = south[step, 1, pl.ds(x, 1), :]
-                curl_x = (hz - down_y(hz, sz_row)) - (hy - down_z(hy))
-                curl_y = (hx - down_z(hx)) - (hz - hz_prev)
-                curl_z = (hy - hy_prev) - (hx - down_y(hx, sx_row))
+            skip_magnetic = adjoint and step == 0
+            if not skip_magnetic:
+                ey = load_e(step, 1, 0)
+                ez = load_e(step, 2, 0)
+                for x in range(size_x):
+                    ex = load_e(step, 0, x)
+                    if x + 1 < size_x:
+                        ey_next = load_e(step, 1, x + 1)
+                        ez_next = load_e(step, 2, x + 1)
+                    else:
+                        ey_next = east[step, 0]
+                        ez_next = east[step, 1]
+                    nx_row = north[step, 0, x : x + 1, :]
+                    nz_row = north[step, 1, x : x + 1, :]
+                    curl_x = (up_y(ez, nz_row) - ez) - (up_z(ey) - ey)
+                    curl_y = (up_z(ex) - ex) - (ez_next - ez)
+                    curl_z = (ey_next - ey) - (up_y(ex, nx_row) - ex)
+                    hx = load_h(step, 0, x) - COURANT * curl_x
+                    hy = load_h(step, 1, x) - COURANT * curl_y
+                    hz = load_h(step, 2, x) - COURANT * curl_z
+                    store_h(0, x, hx)
+                    store_h(1, x, hy)
+                    store_h(2, x, hz)
+                    ys_h[step, 0, x : x + 1, :] = hx[size_y - 1 : size_y, :]
+                    ys_h[step, 1, x : x + 1, :] = hz[size_y - 1 : size_y, :]
+                    if x == size_x - 1:
+                        xs_h[step, 0] = hy
+                        xs_h[step, 1] = hz
+                    ey, ez = ey_next, ez_next
+                swap(
+                    xs_h.at[step], west.at[step], ys_h.at[step], south.at[step], 4 * step + 2,
+                    lax.rem(px + 1, span_x), lax.rem(py + 1, span_y),
+                    has_east, has_north, has_west, has_south,
+                )
+
+            hy_prev = None if skip_magnetic else west[step, 0]
+            hz_prev = None if skip_magnetic else west[step, 1]
+            for x in range(size_x):
+                if skip_magnetic:
+                    curl_x = curl_y = curl_z = zero_slab
+                else:
+                    hx = load_h(step + 1, 0, x)
+                    hy = load_h(step + 1, 1, x)
+                    hz = load_h(step + 1, 2, x)
+                    sx_row = south[step, 0, x : x + 1, :]
+                    sz_row = south[step, 1, x : x + 1, :]
+                    curl_x = (hz - down_y(hz, sz_row)) - (hy - down_z(hy))
+                    curl_y = (hx - down_z(hx)) - (hz - hz_prev)
+                    curl_z = (hy - hy_prev) - (hx - down_y(hx, sx_row))
+                    hy_prev, hz_prev = hy, hz
                 if adjoint:
                     curl_x = curl_x - drv[step, 0, x]
                     curl_y = curl_y - drv[step, 1, x]
@@ -245,20 +252,11 @@
                     before = zero_slab if step == 0 else acc[x]
                     acc[x] = before - product * scale
                 if step + 1 < NT:
-                    ys_e[step + 1, 0, pl.ds(x, 1), :] = ex[0:1, :]
-                    ys_e[step + 1, 1, pl.ds(x, 1), :] = ez[0:1, :]
-                return ey, ez
-
-            ey_first, ez_first = electric(0, west[step, 0], west[step, 1])
-            if step + 1 < NT:
-                xs_e[step + 1, 0] = ey_first
-                xs_e[step + 1, 1] = ez_first
-
-            def electric_body(x, carry, step=step):
-                electric(x, load_h(step + 1, 1, x - 1), load_h(step + 1, 2, x - 1))
-                return carry
-
-            lax.fori_loop(1, size_x, electric_body, 0, unroll=True)
+                    ys_e[step + 1, 0, x : x + 1, :] = ex[0:1, :]
+                    ys_e[step + 1, 1, x : x + 1, :] = ez[0:1, :]
+                    if x == 0:
+                        xs_e[step + 1, 0] = ey
+                        xs_e[step + 1, 1] = ez
 
     rim_x = pltpu.VMEM((NT, 2, size_y, size_z), jnp.float32)
     rim_y = pltpu.VMEM((NT, 2, size_x, size_z), jnp.float32)

time: 202 us -> 197 us (0.975)
  Pallas kernels: 161 us -> 156 us
    pallas_call x2, Pallas kernels: 66.1 us -> 62.6 us  [run_leaps(): pl.pallas_call(kernel, out_shape=out_shape, in_specs=[pl.BlockSpec(memory...]
where the time goes in v5:
time: 197 us; the launch traced here: 196 us
  Pallas kernels  156 us (79%)
  other arithmetic  17.7 us (9%)
  local copies, waits for them, and re-layouts  12 us (6%)
  matrix products  9.18 us (5%)
    pallas_call x4, Pallas kernels, exchange(): pl.pallas_call(kernel, out_shape=jax.ShapeDtypeStruct((count,) + tuple(pi...  64.6 us
    pallas_call x2, Pallas kernels, run_leaps(): pl.pallas_call(kernel, out_shape=out_shape, in_specs=[pl.BlockSpec(memory...  62.6 us
    pallas_call x1, Pallas kernels, focal_rows(): pl.pallas_call(kernel, out_shape=(jax.ShapeDtypeStruct((rows, width), jnp...  28.9 us
    dot_general x16, matrix products, contract(): jnp.einsum(pattern, first_op, second_op, precision=lax.Precision.HIGHEST)  7.68 us

profile of v5, /device:TPU:1, one launch (start us, length us, event | category | flops | bytes accessed | tf_op | source)
XLA Modules:
  0.0 196.1 jit_solution(4864823841917162354)
XLA Ops:
  3.8 0.8 select_reduce_fusion
  5.3 1.0 fusion.13
  6.3 20.7 %shard_map.94 = f32[128,2,18]{2,1,0:T(2,128)} custom-call(f32[128,2,18]{2,1,0:T(2,128)} %bitcast.135), custom_call_target="tpu_custom_call" | custom-call | tf_op jit(solution)/shard_map/pallas_call | solution.py:360
  27.0 1.0 mul.173
  28.1 1.0 slice_convert_fusion
  30.1 2.0 %add_divide_fusion.refs_1_.refs_2_ = f32[32,32,128]{2,1,0:T(8,128)} fusion(f32[32,32,128]{2,1,0:T(8,128)} %param.8, f32[128]{0:T(128)S(1)} %and_convert_fusion, f32[32,32]{1,0:T(8,128)S(1)} %convolution_multiply_fusion), kind=kLoop, calls=%fused_computation.20 | loop fusion | flops 393216 | bytes 1053184 | tf_op jit(solution)/shard_map/div | solution.py:497
  32.2 34.7 %shard_map.95 = (f32[6,32,32,128]{3,2,1,0:T(8,128)}, f32[4,3,32,32,128]{4,3,2,1,0:T(8,128)}) custom-call(f32[6,32,32,128]{3,2,1,0:T(8,128)} %refs_0_.3, f32[32,32,128]{2,1,0:T(8,128)} %add_divide_fusion.refs_1_.refs_2_), custom_call_target="tpu_custom_call" | custom-call | tf_op jit(solution)/shard_map/pallas_call | solution.py:280
  66.9 3.3 %multiply_add_fusion = (f32[1,2,32,32,1]{4,3,2,1,0:T(8,128)S(1)}, f32[1,2,32,32,1]{4,3,2,1,0:T(8,128)S(1)}) fusion(f32[4,3,32,32,128]{4,3,2,1,0:T(8,128)} %get-tuple-element.8.refs_1_), kind=kLoop, calls=%fused_computation.17 | loop fusion | flops 30720 | bytes 49152 | tf_op jit(solution)/shard_map/add | solution.py:503
  73.6 1.1 reshape.161.x_ref
  74.7 9.2 %shard_map.96 = f32[8,32,128]{2,1,0:T(8,128)} custom-call(f32[8,32,128]{2,1,0:T(8,128)} %reshape.161.x_ref), custom_call_target="tpu_custom_call" | custom-call | tf_op jit(solution)/shard_map/pallas_call | solution.py:360
  83.9 0.9 reduce_sum.58
  86.9 0.7 reshape.163.x_ref
  87.6 28.9 %shard_map.97 = (f32[8,256]{1,0:T(8,128)}, f32[16,8,256]{2,1,0:T(8,128)}) custom-call(f32[16,8,256]{2,1,0:T(8,128)} %reshape.163.x_ref, f32[8,256]{1,0:T(8,128)} %reshape.164.t_ref), custom_call_target="tpu_custom_call" | custom-call | tf_op jit(solution)/shard_map/pallas_call | solution.py:425
  116.5 0.8 mul.196
  117.9 1.0 reshape.165
  121.4 6.7 %shard_map.98 = f32[8,32,128]{2,1,0:T(8,128)} custom-call(f32[32,128]{1,0:T(8,128)} %reshape.167.x_ref), custom_call_target="tpu_custom_call" | custom-call | tf_op jit(solution)/shard_map/pallas_call | solution.py:360
  128.1 1.3 reshape.183
  131.4 2.7 %broadcast_select_fusion.refs_3_ = f32[4,2,32,32,128]{4,3,2,1,0:T(8,128)} fusion(f32[4,2,32,32]{3,2,1,0:T(8,128)S(1)} %copy.69, pred[128]{0:T(512)(128)(4,1)S(1)} %iota_compare_fusion.8), kind=kLoop, calls=%fused_computation.1 | loop fusion | flops 1048576 | bytes 4227200 | tf_op jit(solution)/shard_map/jit(_where)/select_n | solution.py:567
  134.0 27.9 %shard_map.99 = f32[32,32,128]{2,1,0:T(8,128)} custom-call(f32[6,32,32,128]{3,2,1,0:T(8,128)} %refs_0_.3, f32[4,3,32,32,128]{4,3,2,1,0:T(8,128)} %get-tuple-element.8.refs_1_, f32[32,32,128]{2,1,0:T(8,128)} %add_divide_fusion.refs_1_.refs_2_, f32[4,2,32,32,128]{4,3,2,1,0:T(8,128)} %broadcast_select_fusion.refs_3_), custom_call_target="tpu_custom_call" | custom-call | tf_op jit(solution)/shard_map/pallas_call | solution.py:280
  161.9 1.4 slice_reduce_fusion
  163.8 0.9 reshape_reshape.3.x_ref
  164.7 28.0 %shard_map.100 = f32[128,2,16]{2,1,0:T(2,128)} custom-call(f32[128,2,16]{2,1,0:T(2,128)} %reshape_reshape.3.x_ref), custom_call_target="tpu_custom_call" | custom-call | tf_op jit(solution)/shard_map/pallas_call | solution.py:360
  192.7 1.2 fusion.5
  194.4 1.7 copy.90
  (68 shorter events, 16.1 us)
Async XLA Ops:
  0.6 1.0 copy-start
  134.0 58.6 %copy-start.2 = (f32[128,16]{0,1:T(8,128)S(1)}, f32[128,16]{0,1:T(8,128)}, u32[]{:S(2)}) copy-start(f32[128,16]{0,1:T(8,128)} %param.11) | copy-start | bytes 24580
  134.0 60.4 %copy-start.1 = (f32[6,32,32,128]{3,2,1,0:T(8,128)S(1)}, f32[6,32,32,128]{3,2,1,0:T(8,128)}, u32[]{:S(2)}) copy-start(f32[6,32,32,128]{3,2,1,0:T(8,128)} %get-tuple-element.26) | copy-start | bytes 9437188

commit v6 on v4

--- a/solution.py
+++ b/solution.py
@@ -63,8 +63,13 @@
     span_x = lax.axis_size("gx")
     span_y = lax.axis_size("gy")
     size_x, size_y, size_z = inv_eps.shape
+    half = size_x // 2
     adjoint = history is not None
     mesh_id = pl.DeviceIdType.MESH
+    order_h = list(range(half - 1, size_x - 1)) + list(range(0, half - 1)) + [size_x - 1]
+    order_e = list(range(half - 1, size_x - 1)) + list(range(1, half - 1)) + [size_x - 1, 0]
+    slot_h = {x: i for i, x in enumerate(order_h)}
+    slot_e = {x: i for i, x in enumerate(order_e)}
 
     def kernel(*refs):
         refs = list(refs)
@@ -91,9 +96,18 @@
         has_west = px > 0
         has_north = py < span_y - 1
         has_south = py > 0
+        west_dev = (lax.rem(px + span_x - 1, span_x), py)
+        east_dev = (lax.rem(px + 1, span_x), py)
+        south_dev = (px, lax.rem(py + span_y - 1, span_y))
+        north_dev = (px, lax.rem(py + 1, span_y))
         zero_slab = jnp.zeros((size_y, size_z), jnp.float32)
         iy = lax.broadcasted_iota(jnp.int32, (size_y, size_z), 0)
         iz = lax.broadcasted_iota(jnp.int32, (size_y, size_z), 1)
+
+        for flag, buf in ((has_east, east), (has_north, north), (has_west, west), (has_south, south)):
+            @pl.when(jnp.logical_not(flag))
+            def _(buf=buf):
+                buf[...] = jnp.zeros(buf.shape, jnp.float32)
 
         def up_y(slab, row):
             return jnp.where(iy == size_y - 1, row, pltpu.roll(slab, size_y - 1, 0))
@@ -123,8 +137,10 @@
                     final[comp, x] = value
 
         def load_h(step, comp, x):
+            if adjoint and step <= 1:
+                return zero_slab
             if step == 0:
-                return zero_slab if adjoint else f_in[3 + comp, x]
+                return f_in[3 + comp, x]
             return h_state[comp, x] if adjoint else final[3 + comp, x]
 
         def store_h(comp, x, value):
@@ -136,132 +152,176 @@
         def forward_e(n, comp, x):
             return f_in[comp, x] if n == 0 else hist[n - 1, comp, x]
 
-        def swap(src_x, dst_x, src_y, dst_y, sem, to_x, to_y, sends_x, sends_y, gets_x, gets_y):
-            copy_x = pltpu.make_async_remote_copy(
-                src_ref=src_x, dst_ref=dst_x, send_sem=ssem.at[sem], recv_sem=rsem.at[sem],
-                device_id=(to_x, py), device_id_type=mesh_id,
+        sent = []
+
+        def link(src, dst, sem, device, sends):
+            copy = pltpu.make_async_remote_copy(
+                src_ref=src, dst_ref=dst, send_sem=ssem.at[sem], recv_sem=rsem.at[sem],
+                device_id=device, device_id_type=mesh_id,
             )
-            copy_y = pltpu.make_async_remote_copy(
-                src_ref=src_y, dst_ref=dst_y, send_sem=ssem.at[sem + 1], recv_sem=rsem.at[sem + 1],
-                device_id=(px, to_y), device_id_type=mesh_id,
+            pl.when(sends)(copy.start)
+            sent.append((copy, sends))
+            return copy
+
+        def wait_for(src, dst, sem, device, gets):
+            copy = pltpu.make_async_remote_copy(
+                src_ref=src, dst_ref=dst, send_sem=ssem.at[sem], recv_sem=rsem.at[sem],
+                device_id=device, device_id_type=mesh_id,
             )
-            pl.when(sends_x)(copy_x.start)
-            pl.when(sends_y)(copy_y.start)
-
-            @pl.when(jnp.logical_not(gets_x))
-            def _():
-                dst_x[...] = jnp.zeros(dst_x.shape, jnp.float32)
-
-            @pl.when(jnp.logical_not(gets_y))
-            def _():
-                dst_y[...] = jnp.zeros(dst_y.shape, jnp.float32)
-
-            pl.when(gets_x)(copy_x.wait_recv)
-            pl.when(gets_y)(copy_y.wait_recv)
-            pl.when(sends_x)(copy_x.wait_send)
-            pl.when(sends_y)(copy_y.wait_send)
+            pl.when(gets)(copy.wait_recv)
+
+        def send_e_rows(step, chunk):
+            link(ys_e.at[step, chunk], north.at[step, chunk], 6 * step + chunk, south_dev, has_south)
+
+        def send_e_slab(step):
+            link(xs_e.at[step], east.at[step], 6 * step + 2, west_dev, has_west)
+
+        def get_e_rows(step, chunk):
+            wait_for(ys_e.at[step, chunk], north.at[step, chunk], 6 * step + chunk, north_dev, has_north)
+
+        def get_e_slab(step):
+            wait_for(xs_e.at[step], east.at[step], 6 * step + 2, east_dev, has_east)
+
+        def send_h_rows(step, chunk):
+            link(ys_h.at[step, chunk], south.at[step, chunk], 6 * step + 3 + chunk, north_dev, has_north)
+
+        def send_h_slab(step):
+            link(xs_h.at[step], west.at[step], 6 * step + 5, east_dev, has_east)
+
+        def get_h_rows(step, chunk):
+            wait_for(ys_h.at[step, chunk], south.at[step, chunk], 6 * step + 3 + chunk, south_dev, has_south)
+
+        def get_h_slab(step):
+            wait_for(xs_h.at[step], west.at[step], 6 * step + 5, west_dev, has_west)
+
+        def e_row_ref(buf, step, comp, x):
+            slot = slot_e[x]
+            return buf[step, slot // half, comp, pl.ds(slot % half, 1), :]
+
+        def h_row_ref(buf, step, comp, x):
+            slot = slot_h[x]
+            return buf[step, slot // half, comp, pl.ds(slot % half, 1), :]
+
+        def stage_e_rows(step, x, ex, ez):
+            slot = slot_e[x]
+            ys_e[step, slot // half, 0, pl.ds(slot % half, 1), :] = ex[0:1, :]
+            ys_e[step, slot // half, 1, pl.ds(slot % half, 1), :] = ez[0:1, :]
 
         if not adjoint:
             xs_e[0, 0] = f_in[1, 0]
             xs_e[0, 1] = f_in[2, 0]
-
-            def stage_first(x, carry):
-                ys_e[0, 0, pl.ds(x, 1), :] = f_in[0, x][0:1, :]
-                ys_e[0, 1, pl.ds(x, 1), :] = f_in[2, x][0:1, :]
-                return carry
-
-            lax.fori_loop(0, size_x, stage_first, 0)
-
-        for step in range(NT):
-            if step == 0 and adjoint:
-                east[0] = jnp.zeros(east.shape[1:], jnp.float32)
-                north[0] = jnp.zeros(north.shape[1:], jnp.float32)
+            for x in order_e:
+                stage_e_rows(0, x, f_in[0, x], f_in[2, x])
+            send_e_rows(0, 0)
+            send_e_rows(0, 1)
+            send_e_slab(0)
+
+        def magnetic(step, x):
+            ex = load_e(step, 0, x)
+            ey = load_e(step, 1, x)
+            ez = load_e(step, 2, x)
+            if x + 1 < size_x:
+                ey_next = load_e(step, 1, x + 1)
+                ez_next = load_e(step, 2, x + 1)
             else:
-                swap(
-                    xs_e.at[step], east.at[step], ys_e.at[step], north.at[step], 4 * step,
-                    lax.rem(px + span_x - 1, span_x), lax.rem(py + span_y - 1, span_y),
-                    has_west, has_south, has_east, has_north,
-                )
-
-            def magnetic(x, ey_next, ez_next, step=step):
-                ex = load_e(step, 0, x)
-                ey = load_e(step, 1, x)
-                ez = load_e(step, 2, x)
-                nx_row = north[step, 0, pl.ds(x, 1), :]
-                nz_row = north[step, 1, pl.ds(x, 1), :]
-                curl_x = (up_y(ez, nz_row) - ez) - (up_z(ey) - ey)
-                curl_y = (up_z(ex) - ex) - (ez_next - ez)
-                curl_z = (ey_next - ey) - (up_y(ex, nx_row) - ex)
-                hx = load_h(step, 0, x) - COURANT * curl_x
-                hy = load_h(step, 1, x) - COURANT * curl_y
-                hz = load_h(step, 2, x) - COURANT * curl_z
-                store_h(0, x, hx)
-                store_h(1, x, hy)
-                store_h(2, x, hz)
-                ys_h[step, 0, pl.ds(x, 1), :] = hx[size_y - 1 : size_y, :]
-                ys_h[step, 1, pl.ds(x, 1), :] = hz[size_y - 1 : size_y, :]
-                return hy, hz
-
-            def magnetic_body(x, carry, step=step):
-                magnetic(x, load_e(step, 1, x + 1), load_e(step, 2, x + 1))
-                return carry
-
-            lax.fori_loop(0, size_x - 1, magnetic_body, 0, unroll=True)
-            hy_last, hz_last = magnetic(size_x - 1, east[step, 0], east[step, 1])
-            xs_h[step, 0] = hy_last
-            xs_h[step, 1] = hz_last
-            swap(
-                xs_h.at[step], west.at[step], ys_h.at[step], south.at[step], 4 * step + 2,
-                lax.rem(px + 1, span_x), lax.rem(py + 1, span_y),
-                has_east, has_north, has_west, has_south,
-            )
-
-            def electric(x, hy_prev, hz_prev, step=step):
+                ey_next = east[step, 0]
+                ez_next = east[step, 1]
+            nx_row = e_row_ref(north, step, 0, x)
+            nz_row = e_row_ref(north, step, 1, x)
+            curl_x = (up_y(ez, nz_row) - ez) - (up_z(ey) - ey)
+            curl_y = (up_z(ex) - ex) - (ez_next - ez)
+            curl_z = (ey_next - ey) - (up_y(ex, nx_row) - ex)
+            hx = load_h(step, 0, x) - COURANT * curl_x
+            hy = load_h(step, 1, x) - COURANT * curl_y
+            hz = load_h(step, 2, x) - COURANT * curl_z
+            store_h(0, x, hx)
+            store_h(1, x, hy)
+            store_h(2, x, hz)
+            slot = slot_h[x]
+            ys_h[step, slot // half, 0, pl.ds(slot % half, 1), :] = hx[size_y - 1 : size_y, :]
+            ys_h[step, slot // half, 1, pl.ds(slot % half, 1), :] = hz[size_y - 1 : size_y, :]
+            if x == size_x - 1:
+                xs_h[step, 0] = hy
+                xs_h[step, 1] = hz
+
+        def electric(step, x, skip_magnetic):
+            if skip_magnetic:
+                curl_x = curl_y = curl_z = zero_slab
+            else:
                 hx = load_h(step + 1, 0, x)
                 hy = load_h(step + 1, 1, x)
                 hz = load_h(step + 1, 2, x)
-                sx_row = south[step, 0, pl.ds(x, 1), :]
-                sz_row = south[step, 1, pl.ds(x, 1), :]
+                if x > 0:
+                    hy_prev = load_h(step + 1, 1, x - 1)
+                    hz_prev = load_h(step + 1, 2, x - 1)
+                else:
+                    hy_prev = west[step, 0]
+                    hz_prev = west[step, 1]
+                sx_row = h_row_ref(south, step, 0, x)
+                sz_row = h_row_ref(south, step, 1, x)
                 curl_x = (hz - down_y(hz, sz_row)) - (hy - down_z(hy))
                 curl_y = (hx - down_z(hx)) - (hz - hz_prev)
                 curl_z = (hy - hy_prev) - (hx - down_y(hx, sx_row))
-                if adjoint:
-                    curl_x = curl_x - drv[step, 0, x]
-                    curl_y = curl_y - drv[step, 1, x]
-                scale = eps_ref[x]
-                ex = load_e(step, 0, x) + COURANT * curl_x * scale
-                ey = load_e(step, 1, x) + COURANT * curl_y * scale
-                ez = load_e(step, 2, x) + COURANT * curl_z * scale
-                store_e(step, 0, x, ex)
-                store_e(step, 1, x, ey)
-                store_e(step, 2, x, ez)
-                if adjoint:
-                    moment = NT - step
-                    product = (
-                        ex * (forward_e(moment, 0, x) - forward_e(moment - 1, 0, x))
-                        + ey * (forward_e(moment, 1, x) - forward_e(moment - 1, 1, x))
-                        + ez * (forward_e(moment, 2, x) - forward_e(moment - 1, 2, x))
-                    )
-                    before = zero_slab if step == 0 else acc[x]
-                    acc[x] = before - product * scale
-                if step + 1 < NT:
-                    ys_e[step + 1, 0, pl.ds(x, 1), :] = ex[0:1, :]
-                    ys_e[step + 1, 1, pl.ds(x, 1), :] = ez[0:1, :]
-                return ey, ez
-
-            ey_first, ez_first = electric(0, west[step, 0], west[step, 1])
+            if adjoint:
+                curl_x = curl_x - drv[step, 0, x]
+                curl_y = curl_y - drv[step, 1, x]
+            scale = eps_ref[x]
+            ex = load_e(step, 0, x) + COURANT * curl_x * scale
+            ey = load_e(step, 1, x) + COURANT * curl_y * scale
+            ez = load_e(step, 2, x) + COURANT * curl_z * scale
+            store_e(step, 0, x, ex)
+            store_e(step, 1, x, ey)
+            store_e(step, 2, x, ez)
+            if adjoint:
+                moment = NT - step
+                product = (
+                    ex * (forward_e(moment, 0, x) - forward_e(moment - 1, 0, x))
+                    + ey * (forward_e(moment, 1, x) - forward_e(moment - 1, 1, x))
+                    + ez * (forward_e(moment, 2, x) - forward_e(moment - 1, 2, x))
+                )
+                before = zero_slab if step == 0 else acc[x]
+                acc[x] = before - product * scale
             if step + 1 < NT:
-                xs_e[step + 1, 0] = ey_first
-                xs_e[step + 1, 1] = ez_first
-
-            def electric_body(x, carry, step=step):
-                electric(x, load_h(step + 1, 1, x - 1), load_h(step + 1, 2, x - 1))
-                return carry
-
-            lax.fori_loop(1, size_x, electric_body, 0, unroll=True)
+                stage_e_rows(step + 1, x, ex, ez)
+                if x == 0:
+                    xs_e[step + 1, 0] = ey
+                    xs_e[step + 1, 1] = ez
+
+        for step in range(NT):
+            skip_magnetic = adjoint and step == 0
+            if not skip_magnetic:
+                get_e_rows(step, 0)
+                for x in order_h[:half]:
+                    magnetic(step, x)
+                send_h_rows(step, 0)
+                get_e_rows(step, 1)
+                for x in order_h[half:-1]:
+                    magnetic(step, x)
+                get_e_slab(step)
+                magnetic(step, order_h[-1])
+                send_h_rows(step, 1)
+                send_h_slab(step)
+                get_h_rows(step, 0)
+            for x in order_e[:half]:
+                electric(step, x, skip_magnetic)
+            if step + 1 < NT:
+                send_e_rows(step + 1, 0)
+            if not skip_magnetic:
+                get_h_rows(step, 1)
+            for x in order_e[half:-1]:
+                electric(step, x, skip_magnetic)
+            if not skip_magnetic:
+                get_h_slab(step)
+            electric(step, order_e[-1], skip_magnetic)
+            if step + 1 < NT:
+                send_e_rows(step + 1, 1)
+                send_e_slab(step + 1)
+
+        for copy, sends in sent:
+            pl.when(sends)(copy.wait_send)
 
     rim_x = pltpu.VMEM((NT, 2, size_y, size_z), jnp.float32)
-    rim_y = pltpu.VMEM((NT, 2, size_x, size_z), jnp.float32)
+    rim_y = pltpu.VMEM((NT, 2, 2, half, size_z), jnp.float32)
     field_shape = (size_x, size_y, size_z)
     if adjoint:
         operands = [fields, history, inv_eps, drive]
@@ -286,8 +346,8 @@
         out_specs=out_specs,
         scratch_shapes=state + [
             rim_x, rim_y, rim_x, rim_y, rim_x, rim_y, rim_x, rim_y,
-            pltpu.SemaphoreType.DMA((4 * NT,)),
-            pltpu.SemaphoreType.DMA((4 * NT,)),
+            pltpu.SemaphoreType.DMA((6 * NT,)),
+            pltpu.SemaphoreType.DMA((6 * NT,)),
         ],
         compiler_params=pltpu.CompilerParams(
             collective_id=tag, has_side_effects=True, vmem_limit_bytes=56 * 1024 * 1024

time: 202 us -> 187 us (0.926)
  Pallas kernels: 161 us -> 147 us
    pallas_call x2, Pallas kernels: 66.1 us -> 58.2 us  [run_leaps(): pl.pallas_call(kernel, out_shape=out_shape, in_specs=[pl.BlockSpec(memory...]
    pallas_call x1, Pallas kernels: 28.9 us -> 25.2 us  [focal_rows(): pl.pallas_call(kernel, out_shape=(jax.ShapeDtypeStruct((rows, width), jnp...]
    pallas_call x4, Pallas kernels: 66.1 us -> 63.2 us  [exchange(): pl.pallas_call(kernel, out_shape=jax.ShapeDtypeStruct((count,) + tuple(pi...]
where the time goes in v6:
time: 187 us
  Pallas kernels  147 us (79%)
  other arithmetic  17.7 us (9%)
  local copies, waits for them, and re-layouts  12.2 us (7%)
  matrix products  9.18 us (5%)
    pallas_call x4, Pallas kernels, exchange(): pl.pallas_call(kernel, out_shape=jax.ShapeDtypeStruct((count,) + tuple(pi...  63.2 us
    pallas_call x2, Pallas kernels, run_leaps(): pl.pallas_call(kernel, out_shape=out_shape, in_specs=[pl.BlockSpec(memory...  58.2 us
    pallas_call x1, Pallas kernels, focal_rows(): pl.pallas_call(kernel, out_shape=(jax.ShapeDtypeStruct((rows, width), jnp...  25.2 us
    dot_general x16, matrix products, contract(): jnp.einsum(pattern, first_op, second_op, precision=lax.Precision.HIGHEST)  7.68 us

profile of v6, /device:TPU:1, one launch (start us, length us, event | category | flops | bytes accessed | tf_op | source)
XLA Modules:
  0.0 186.8 jit_solution(16960864824643734098)
XLA Ops:
  3.8 0.8 select_reduce_fusion
  5.3 1.0 fusion.13
  6.3 20.7 %shard_map.94 = f32[128,2,18]{2,1,0:T(2,128)} custom-call(f32[128,2,18]{2,1,0:T(2,128)} %bitcast.135), custom_call_target="tpu_custom_call" | custom-call | tf_op jit(solution)/shard_map/pallas_call | solution.py:422
  27.0 1.0 mul.173
  28.1 1.0 slice_convert_fusion
  30.1 2.0 %add_divide_fusion.refs_1_.refs_2_ = f32[32,32,128]{2,1,0:T(8,128)} fusion(f32[32,32,128]{2,1,0:T(8,128)} %param.8, f32[128]{0:T(128)S(1)} %and_convert_fusion, f32[32,32]{1,0:T(8,128)S(1)} %convolution_multiply_fusion), kind=kLoop, calls=%fused_computation.20 | loop fusion | flops 393216 | bytes 1053184 | tf_op jit(solution)/shard_map/div | solution.py:559
  32.2 32.5 %shard_map.95 = (f32[6,32,32,128]{3,2,1,0:T(8,128)}, f32[4,3,32,32,128]{4,3,2,1,0:T(8,128)}) custom-call(f32[6,32,32,128]{3,2,1,0:T(8,128)} %refs_0_.3, f32[32,32,128]{2,1,0:T(8,128)} %add_divide_fusion.refs_1_.refs_2_), custom_call_target="tpu_custom_call" | custom-call | tf_op jit(solution)/shard_map/pallas_call | solution.py:342
  64.7 3.3 %multiply_add_fusion = (f32[1,2,32,32,1]{4,3,2,1,0:T(8,128)S(1)}, f32[1,2,32,32,1]{4,3,2,1,0:T(8,128)S(1)}) fusion(f32[4,3,32,32,128]{4,3,2,1,0:T(8,128)} %get-tuple-element.8.refs_1_), kind=kLoop, calls=%fused_computation.17 | loop fusion | flops 30720 | bytes 49152 | tf_op jit(solution)/shard_map/add | solution.py:565
  71.4 1.1 reshape.161.x_ref
  72.5 9.6 %shard_map.96 = f32[8,32,128]{2,1,0:T(8,128)} custom-call(f32[8,32,128]{2,1,0:T(8,128)} %reshape.161.x_ref), custom_call_target="tpu_custom_call" | custom-call | tf_op jit(solution)/shard_map/pallas_call | solution.py:422
  82.1 0.9 reduce_sum.58
  85.1 0.7 reshape.163.x_ref
  85.8 25.2 %shard_map.97 = (f32[8,256]{1,0:T(8,128)}, f32[16,8,256]{2,1,0:T(8,128)}) custom-call(f32[16,8,256]{2,1,0:T(8,128)} %reshape.163.x_ref, f32[8,256]{1,0:T(8,128)} %reshape.164.t_ref), custom_call_target="tpu_custom_call" | custom-call | tf_op jit(solution)/shard_map/pallas_call | solution.py:487
  111.0 0.8 mul.196
  112.4 1.0 reshape.165
  115.9 6.7 %shard_map.98 = f32[8,32,128]{2,1,0:T(8,128)} custom-call(f32[32,128]{1,0:T(8,128)} %reshape.167.x_ref), custom_call_target="tpu_custom_call" | custom-call | tf_op jit(solution)/shard_map/pallas_call | solution.py:422
  122.6 1.6 reshape.183
  126.1 2.7 %broadcast_select_fusion.refs_3_ = f32[4,2,32,32,128]{4,3,2,1,0:T(8,128)} fusion(f32[4,2,32,32]{3,2,1,0:T(8,128)S(1)} %copy.69, pred[128]{0:T(512)(128)(4,1)S(1)} %iota_compare_fusion.8), kind=kLoop, calls=%fused_computation.1 | loop fusion | flops 1048576 | bytes 4227200 | tf_op jit(solution)/shard_map/jit(_where)/select_n | solution.py:629
  128.8 25.6 %shard_map.99 = f32[32,32,128]{2,1,0:T(8,128)} custom-call(f32[6,32,32,128]{3,2,1,0:T(8,128)} %refs_0_.3, f32[4,3,32,32,128]{4,3,2,1,0:T(8,128)} %get-tuple-element.8.refs_1_, f32[32,32,128]{2,1,0:T(8,128)} %add_divide_fusion.refs_1_.refs_2_, f32[4,2,32,32,128]{4,3,2,1,0:T(8,128)} %broadcast_select_fusion.refs_3_), custom_call_target="tpu_custom_call" | custom-call | tf_op jit(solution)/shard_map/pallas_call | solution.py:342
  154.5 1.4 slice_reduce_fusion
  156.3 0.9 reshape_reshape.3.x_ref
  157.2 26.2 %shard_map.100 = f32[128,2,16]{2,1,0:T(2,128)} custom-call(f32[128,2,16]{2,1,0:T(2,128)} %reshape_reshape.3.x_ref), custom_call_target="tpu_custom_call" | custom-call | tf_op jit(solution)/shard_map/pallas_call | solution.py:422
  183.4 1.2 fusion.5
  185.1 1.7 copy.90
  (68 shorter events, 16.1 us)
Async XLA Ops:
  0.6 1.0 copy-start
  128.8 54.6 %copy-start.2 = (f32[128,16]{0,1:T(8,128)S(1)}, f32[128,16]{0,1:T(8,128)}, u32[]{:S(2)}) copy-start(f32[128,16]{0,1:T(8,128)} %param.11) | copy-start | bytes 24580
  128.8 56.3 %copy-start.1 = (f32[6,32,32,128]{3,2,1,0:T(8,128)S(1)}, f32[6,32,32,128]{3,2,1,0:T(8,128)}, u32[]{:S(2)}) copy-start(f32[6,32,32,128]{3,2,1,0:T(8,128)} %get-tuple-element.26) | copy-start | bytes 9437188

commit v7 on v6

--- a/solution.py
+++ b/solution.py
@@ -74,12 +74,13 @@
     def kernel(*refs):
         refs = list(refs)
         if adjoint:
-            f_in, hist, eps_ref, drv, acc = refs[:5]
-            a_hist, h_state = refs[5:7]
-            rest = refs[7:]
+            hist, eps_ref, drv, acc = refs[:4]
+            a_hist, h_state = refs[4:6]
+            rest = refs[6:]
         else:
-            f_in, eps_ref, final, e_hist = refs[:4]
-            rest = refs[4:]
+            f_in, eps_ref, final, chg, mon = refs[:5]
+            a_hist = refs[5]
+            rest = refs[6:]
         east, north, west, south, xs_e, ys_e, xs_h, ys_h, ssem, rsem = rest
         px = lax.axis_index("gx")
         py = lax.axis_index("gy")
@@ -124,17 +125,13 @@
         def load_e(step, comp, x):
             if step == 0:
                 return zero_slab if adjoint else f_in[comp, x]
-            if adjoint:
-                return a_hist[(step - 1) % 2, comp, x]
-            return e_hist[step - 1, comp, x]
+            return a_hist[(step - 1) % 2, comp, x]
 
         def store_e(step, comp, x, value):
-            if adjoint:
+            if step == NT - 1 and not adjoint:
+                final[comp, x] = value
+            else:
                 a_hist[step % 2, comp, x] = value
-            else:
-                e_hist[step, comp, x] = value
-                if step == NT - 1:
-                    final[comp, x] = value
 
         def load_h(step, comp, x):
             if adjoint and step <= 1:
@@ -148,9 +145,6 @@
                 h_state[comp, x] = value
             else:
                 final[3 + comp, x] = value
-
-        def forward_e(n, comp, x):
-            return f_in[comp, x] if n == 0 else hist[n - 1, comp, x]
 
         sent = []
 
@@ -263,30 +257,39 @@
                 curl_y = (hx - down_z(hx)) - (hz - hz_prev)
                 curl_z = (hy - hy_prev) - (hx - down_y(hx, sx_row))
             if adjoint:
-                curl_x = curl_x - drv[step, 0, x]
-                curl_y = curl_y - drv[step, 1, x]
+                to_layer = (ZM - x) % size_z
+                curl_x = curl_x - jnp.where(iz == ZM, pltpu.roll(drv[step, 0], to_layer, 1), 0.0)
+                curl_y = curl_y - jnp.where(iz == ZM, pltpu.roll(drv[step, 1], to_layer, 1), 0.0)
             scale = eps_ref[x]
-            ex = load_e(step, 0, x) + COURANT * curl_x * scale
-            ey = load_e(step, 1, x) + COURANT * curl_y * scale
-            ez = load_e(step, 2, x) + COURANT * curl_z * scale
+            e_old = [load_e(step, comp, x) for comp in range(3)]
+            ex = e_old[0] + COURANT * curl_x * scale
+            ey = e_old[1] + COURANT * curl_y * scale
+            ez = e_old[2] + COURANT * curl_z * scale
             store_e(step, 0, x, ex)
             store_e(step, 1, x, ey)
             store_e(step, 2, x, ez)
             if adjoint:
                 moment = NT - step
                 product = (
-                    ex * (forward_e(moment, 0, x) - forward_e(moment - 1, 0, x))
-                    + ey * (forward_e(moment, 1, x) - forward_e(moment - 1, 1, x))
-                    + ez * (forward_e(moment, 2, x) - forward_e(moment - 1, 2, x))
+                    ex * hist[moment - 1, 0, x]
+                    + ey * hist[moment - 1, 1, x]
+                    + ez * hist[moment - 1, 2, x]
                 )
                 before = zero_slab if step == 0 else acc[x]
                 acc[x] = before - product * scale
+            else:
+                for comp, value in enumerate((ex, ey, ez)):
+                    chg[step, comp, x] = value - e_old[comp]
+                from_layer = (x - ZM) % size_z
+                for comp, value in enumerate((ex, ey)):
+                    packed[comp] = jnp.where(iz == x, pltpu.roll(value, from_layer, 1), packed[comp])
             if step + 1 < NT:
                 stage_e_rows(step + 1, x, ex, ez)
                 if x == 0:
                     xs_e[step + 1, 0] = ey
                     xs_e[step + 1, 1] = ez
 
+        packed = [zero_slab, zero_slab]
         for step in range(NT):
             skip_magnetic = adjoint and step == 0
             if not skip_magnetic:
@@ -316,6 +319,9 @@
             if step + 1 < NT:
                 send_e_rows(step + 1, 1)
                 send_e_slab(step + 1)
+            if not adjoint:
+                mon[step, 0] = packed[0]
+                mon[step, 1] = packed[1]
 
         for copy, sends in sent:
             pl.when(sends)(copy.wait_send)
@@ -324,7 +330,7 @@
     rim_y = pltpu.VMEM((NT, 2, 2, half, size_z), jnp.float32)
     field_shape = (size_x, size_y, size_z)
     if adjoint:
-        operands = [fields, history, inv_eps, drive]
+        operands = [history, inv_eps, drive]
         out_shape = jax.ShapeDtypeStruct(field_shape, jnp.float32)
         out_specs = pl.BlockSpec(memory_space=pltpu.VMEM)
         state = [
@@ -336,9 +342,10 @@
         out_shape = (
             jax.ShapeDtypeStruct((6,) + field_shape, jnp.float32),
             jax.ShapeDtypeStruct((NT, 3) + field_shape, jnp.float32),
+            jax.ShapeDtypeStruct((NT, 2, size_y, size_z), jnp.float32),
         )
-        out_specs = (pl.BlockSpec(memory_space=pltpu.VMEM),) * 2
-        state = []
+        out_specs = (pl.BlockSpec(memory_space=pltpu.VMEM),) * 3
+        state = [pltpu.VMEM((2, 3) + field_shape, jnp.float32)]
     return pl.pallas_call(
         kernel,
         out_shape=out_shape,
@@ -557,11 +564,12 @@
     layers = ((z_index >= ZM - ZP) & (z_index < ZM)).astype(jnp.float32)
     permittivity = eps_background + DELTA_EPS * filling[:, :, None] * layers[None, None, :]
     inv_eps = 1.0 / permittivity
-    final_fields, e_steps = run_leaps(fields, inv_eps, None, None, 10)
+    final_fields, e_changes, packed_mon = run_leaps(fields, inv_eps, None, None, 10)
+    packed_mon = packed_mon[:, :, :, :TILE].swapaxes(2, 3)
     mon_re = jnp.zeros((2, TILE, TILE), jnp.float32)
     mon_im = jnp.zeros((2, TILE, TILE), jnp.float32)
     for moment in range(1, NT + 1):
-        monitor = e_steps[moment - 1, 0:2, :, :, ZM]
+        monitor = packed_mon[moment - 1]
         mon_re = mon_re + math.cos(ANGULAR_STEP * moment) * monitor
         mon_im = mon_im - math.sin(ANGULAR_STEP * moment) * monitor
     norm_scale = (TILE * span_x * TILE * span_y) ** (-0.5)
@@ -624,10 +632,9 @@
             + math.sin(ANGULAR_STEP * source_step) * back_im
         )
         drives.append(adj_drive)
-    drive = jnp.stack(drives)
-    z_index = jnp.arange(fields.shape[3], dtype=jnp.int32)
-    drive = jnp.where(z_index == ZM, drive[..., None], 0.0)
-    grad_eps = run_leaps(fields, inv_eps, e_steps, drive, 11)
+    drive = jnp.stack(drives).swapaxes(2, 3)
+    drive = jnp.pad(drive, ((0, 0), (0, 0), (0, 0), (0, fields.shape[3] - TILE)))
+    grad_eps = run_leaps(None, inv_eps, e_changes, drive, 11)
     column_grad = jnp.sum(grad_eps[:, :, ZM - ZP : ZM], axis=2)
     spread = contract("sx,xy->sy", pick_x, column_grad)
     picked = jnp.sum(spread * pick_y, axis=1).reshape(devices * capacity, 16)

time: 187 us -> 181 us (0.968)
  other arithmetic: 17.7 us -> 11 us
    add x1, other arithmetic: 3.32 us -> 0.02 us  [shards(): mon_re = mon_re + math.cos(ANGULAR_STEP * moment) * monitor]
    select_n x1 -> x0, other arithmetic: 2.66 us -> none  [shards(): drive = jnp.where(z_index == ZM, drive[..., None], 0.0)]
    pallas_call x1, Pallas kernels: 25.2 us -> 27.1 us  [focal_rows(): pl.pallas_call(kernel, out_shape=(jax.ShapeDtypeStruct((rows, width), jnp...]
where the time goes in v7:
time: 181 us
  Pallas kernels  147 us (81%)
  local copies, waits for them, and re-layouts  12.4 us (7%)
  other arithmetic  11 us (6%)
  matrix products  9.18 us (5%)
    pallas_call x4, Pallas kernels, exchange(): pl.pallas_call(kernel, out_shape=jax.ShapeDtypeStruct((count,) + tuple(pi...  62.8 us
    pallas_call x2, Pallas kernels, run_leaps(): pl.pallas_call(kernel, out_shape=out_shape, in_specs=[pl.BlockSpec(memory...  57.3 us
    pallas_call x1, Pallas kernels, focal_rows(): pl.pallas_call(kernel, out_shape=(jax.ShapeDtypeStruct((rows, width), jnp...  27.1 us
    dot_general x16, matrix products, contract(): jnp.einsum(pattern, first_op, second_op, precision=lax.Precision.HIGHEST)  7.67 us

profile of v7, /device:TPU:1, one launch (start us, length us, event | category | flops | bytes accessed | tf_op | source)
XLA Modules:
  0.0 180.8 jit_solution(18176022116489633905)
XLA Ops:
  0.6 0.8 fusion.17
  1.6 0.8 select_reduce_fusion
  4.5 1.0 fusion.13
  5.5 20.7 %shard_map.94 = f32[128,2,18]{2,1,0:T(2,128)} custom-call(f32[128,2,18]{2,1,0:T(2,128)} %bitcast.139), custom_call_target="tpu_custom_call" | custom-call | tf_op jit(solution)/shard_map/pallas_call | solution.py:429
  26.2 1.0 slice_convert_fusion
  27.8 1.0 mul.173
  29.3 2.0 %add_divide_fusion.refs_1_ = f32[32,32,128]{2,1,0:T(8,128)} fusion(f32[32,32,128]{2,1,0:T(8,128)} %param.8, f32[128]{0:T(128)S(1)} %and_convert_fusion, f32[32,32]{1,0:T(8,128)S(1)} %convolution_multiply_fusion), kind=kLoop, calls=%fused_computation.17 | loop fusion | flops 393216 | bytes 1053184 | tf_op jit(solution)/shard_map/div | solution.py:566
  31.3 33.6 %shard_map.95 = (f32[6,32,32,128]{3,2,1,0:T(8,128)}, f32[4,3,32,32,128]{4,3,2,1,0:T(8,128)}, f32[4,2,32,128]{3,2,1,0:T(8,128)}) custom-call(f32[6,32,32,128]{3,2,1,0:T(8,128)} %refs_0_.1, f32[32,32,128]{2,1,0:T(8,128)} %add_divide_fusion.refs_1_), custom_call_target="tpu_custom_call" | custom-call | tf_op jit(solution)/shard_map/pallas_call | solution.py:349
  64.9 0.9 slice_bitcast_fusion
  68.1 1.1 reshape.160.x_ref
  69.1 9.2 %shard_map.96 = f32[8,32,128]{2,1,0:T(8,128)} custom-call(f32[8,32,128]{2,1,0:T(8,128)} %reshape.160.x_ref), custom_call_target="tpu_custom_call" | custom-call | tf_op jit(solution)/shard_map/pallas_call | solution.py:429
  78.3 0.9 reduce_sum.58
  81.3 0.7 reshape.162.x_ref
  82.7 27.1 %shard_map.97 = (f32[8,256]{1,0:T(8,128)}, f32[16,8,256]{2,1,0:T(8,128)}) custom-call(f32[16,8,256]{2,1,0:T(8,128)} %reshape.162.x_ref, f32[8,256]{1,0:T(8,128)} %reshape.163.t_ref), custom_call_target="tpu_custom_call" | custom-call | tf_op jit(solution)/shard_map/pallas_call | solution.py:494
  109.8 1.0 reshape.164
  112.6 0.7 reshape.166.x_ref
  113.3 6.7 %shard_map.98 = f32[8,32,128]{2,1,0:T(8,128)} custom-call(f32[32,128]{1,0:T(8,128)} %reshape.166.x_ref), custom_call_target="tpu_custom_call" | custom-call | tf_op jit(solution)/shard_map/pallas_call | solution.py:429
  120.0 1.3 reshape.182
  124.1 23.7 %shard_map.99 = f32[32,32,128]{2,1,0:T(8,128)} custom-call(f32[4,3,32,32,128]{4,3,2,1,0:T(8,128)} %get-tuple-element.11.refs_0_, f32[32,32,128]{2,1,0:T(8,128)} %add_divide_fusion.refs_1_, f32[4,2,32,128]{3,2,1,0:T(8,128)} %pad.4.refs_2_), custom_call_target="tpu_custom_call" | custom-call | tf_op jit(solution)/shard_map/pallas_call | solution.py:349
  147.8 1.4 slice_reduce_fusion
  149.7 0.9 reshape_reshape.3.x_ref
  150.6 26.2 %shard_map.100 = f32[128,2,16]{2,1,0:T(2,128)} custom-call(f32[128,2,16]{2,1,0:T(2,128)} %reshape_reshape.3.x_ref), custom_call_target="tpu_custom_call" | custom-call | tf_op jit(solution)/shard_map/pallas_call | solution.py:429
  176.8 1.2 fusion.5
  179.2 1.7 copy.51
  (67 shorter events, 14.0 us)
Async XLA Ops:
  0.6 81.4 %copy-start = (f32[256,256]{1,0:T(8,128)S(1)}, f32[256,256]{1,0:T(8,128)}, u32[]{:S(2)}) copy-start(f32[256,256]{1,0:T(8,128)} %param.9) | copy-start | bytes 786436
  124.1 52.7 %copy-start.3 = (f32[128,16]{0,1:T(8,128)S(1)}, f32[128,16]{0,1:T(8,128)}, u32[]{:S(2)}) copy-start(f32[128,16]{0,1:T(8,128)} %param.11) | copy-start | bytes 24580
  124.1 54.4 %copy-start.2 = (f32[8,256]{1,0:T(8,128)S(1)}, f32[8,256]{1,0:T(8,128)}, u32[]{:S(2)}) copy-start(f32[8,256]{1,0:T(8,128)} %get-tuple-element.10) | copy-start | bytes 24580
  124.1 55.1 %copy-start.1 = (f32[6,32,32,128]{3,2,1,0:T(8,128)S(1)}, f32[6,32,32,128]{3,2,1,0:T(8,128)}, u32[]{:S(2)}) copy-start(f32[6,32,32,128]{3,2,1,0:T(8,128)} %get-tuple-element.28) | copy-start | bytes 9437188

commit v8 on v7

--- a/solution.py
+++ b/solution.py
@@ -270,16 +270,19 @@
             store_e(step, 2, x, ez)
             if adjoint:
                 moment = NT - step
+                to_layers = (ZM - ZP - ZP * x) % size_z
                 product = (
-                    ex * hist[moment - 1, 0, x]
-                    + ey * hist[moment - 1, 1, x]
-                    + ez * hist[moment - 1, 2, x]
+                    ex * pltpu.roll(hist[moment - 1, 0], to_layers, 1)
+                    + ey * pltpu.roll(hist[moment - 1, 1], to_layers, 1)
+                    + ez * pltpu.roll(hist[moment - 1, 2], to_layers, 1)
                 )
                 before = zero_slab if step == 0 else acc[x]
                 acc[x] = before - product * scale
             else:
+                from_layers = (ZP * x - (ZM - ZP)) % size_z
                 for comp, value in enumerate((ex, ey, ez)):
-                    chg[step, comp, x] = value - e_old[comp]
+                    moved = pltpu.roll(value - e_old[comp], from_layers, 1)
+                    changed[comp] = jnp.where(iz // ZP == x, moved, changed[comp])
                 from_layer = (x - ZM) % size_z
                 for comp, value in enumerate((ex, ey)):
                     packed[comp] = jnp.where(iz == x, pltpu.roll(value, from_layer, 1), packed[comp])
@@ -290,6 +293,7 @@
                     xs_e[step + 1, 1] = ez
 
         packed = [zero_slab, zero_slab]
+        changed = [zero_slab, zero_slab, zero_slab]
         for step in range(NT):
             skip_magnetic = adjoint and step == 0
             if not skip_magnetic:
@@ -322,6 +326,8 @@
             if not adjoint:
                 mon[step, 0] = packed[0]
                 mon[step, 1] = packed[1]
+                for comp in range(3):
+                    chg[step, comp] = changed[comp]
 
         for copy, sends in sent:
             pl.when(sends)(copy.wait_send)
@@ -341,7 +347,7 @@
         operands = [fields, inv_eps]
         out_shape = (
             jax.ShapeDtypeStruct((6,) + field_shape, jnp.float32),
-            jax.ShapeDtypeStruct((NT, 3) + field_shape, jnp.float32),
+            jax.ShapeDtypeStruct((NT, 3, size_y, size_z), jnp.float32),
             jax.ShapeDtypeStruct((NT, 2, size_y, size_z), jnp.float32),
         )
         out_specs = (pl.BlockSpec(memory_space=pltpu.VMEM),) * 3

time: 181 us -> 184 us (1.017)
    pallas_call x1, Pallas kernels: 27.1 us -> 29.8 us  [focal_rows(): pl.pallas_call(kernel, out_shape=(jax.ShapeDtypeStruct((rows, width), jnp...]
    pallas_call x2, Pallas kernels: 57.3 us -> 55.1 us  [run_leaps(): pl.pallas_call(kernel, out_shape=out_shape, in_specs=[pl.BlockSpec(memory...]
where the time goes in v8:
time: 184 us
  Pallas kernels  147 us (80%)
  local copies, waits for them, and re-layouts  13.9 us (8%)
  other arithmetic  11.7 us (6%)
  matrix products  9.91 us (5%)
    pallas_call x4, Pallas kernels, exchange(): pl.pallas_call(kernel, out_shape=jax.ShapeDtypeStruct((count,) + tuple(pi...  62.2 us
    pallas_call x2, Pallas kernels, run_leaps(): pl.pallas_call(kernel, out_shape=out_shape, in_specs=[pl.BlockSpec(memory...  55.1 us
    pallas_call x1, Pallas kernels, focal_rows(): pl.pallas_call(kernel, out_shape=(jax.ShapeDtypeStruct((rows, width), jnp...  29.8 us
    dot_general x16, matrix products, contract(): jnp.einsum(pattern, first_op, second_op, precision=lax.Precision.HIGHEST)  8.4 us

profile of v8, /device:TPU:1, one launch (start us, length us, event | category | flops | bytes accessed | tf_op | source)
XLA Modules:
  0.0 183.7 jit_solution(12065687669375979856)
XLA Ops:
  0.6 0.8 fusion.17
  1.6 0.8 select_reduce_fusion
  4.5 1.0 fusion.13
  5.5 20.7 %shard_map.94 = f32[128,2,18]{2,1,0:T(2,128)} custom-call(f32[128,2,18]{2,1,0:T(2,128)} %bitcast.139), custom_call_target="tpu_custom_call" | custom-call | tf_op jit(solution)/shard_map/pallas_call | solution.py:435
  26.2 1.0 slice_convert_fusion
  27.8 1.0 mul.173
  29.3 2.0 %add_divide_fusion.refs_1_ = f32[32,32,128]{2,1,0:T(8,128)} fusion(f32[32,32,128]{2,1,0:T(8,128)} %param.8, f32[128]{0:T(128)S(1)} %and_convert_fusion, f32[32,32]{1,0:T(8,128)S(1)} %convolution_multiply_fusion), kind=kLoop, calls=%fused_computation.17 | loop fusion | flops 393216 | bytes 1053184 | tf_op jit(solution)/shard_map/div | solution.py:572
  31.4 32.8 %shard_map.95 = (f32[6,32,32,128]{3,2,1,0:T(8,128)}, f32[4,3,32,128]{3,2,1,0:T(8,128)}, f32[4,2,32,128]{3,2,1,0:T(8,128)}) custom-call(f32[6,32,32,128]{3,2,1,0:T(8,128)} %refs_0_.1, f32[32,32,128]{2,1,0:T(8,128)} %add_divide_fusion.refs_1_), custom_call_target="tpu_custom_call" | custom-call | tf_op jit(solution)/shard_map/pallas_call | solution.py:355
  64.1 0.9 slice_bitcast_fusion
  67.3 1.1 reshape.160.x_ref
  68.4 8.1 %shard_map.96 = f32[8,32,128]{2,1,0:T(8,128)} custom-call(f32[8,32,128]{2,1,0:T(8,128)} %reshape.160.x_ref), custom_call_target="tpu_custom_call" | custom-call | tf_op jit(solution)/shard_map/pallas_call | solution.py:435
  76.4 0.9 reduce_sum.58
  80.8 29.8 %shard_map.97 = (f32[8,256]{1,0:T(8,128)}, f32[16,8,256]{2,1,0:T(8,128)}) custom-call(f32[16,8,256]{2,1,0:T(8,128)} %reshape.162.x_ref, f32[8,256]{1,0:T(8,128)} %reshape.163.t_ref), custom_call_target="tpu_custom_call" | custom-call | tf_op jit(solution)/shard_map/pallas_call | solution.py:500
  110.6 1.0 reshape.164
  114.1 6.7 %shard_map.98 = f32[8,32,128]{2,1,0:T(8,128)} custom-call(f32[32,128]{1,0:T(8,128)} %reshape.166.x_ref), custom_call_target="tpu_custom_call" | custom-call | tf_op jit(solution)/shard_map/pallas_call | solution.py:435
  120.8 2.1 %reshape.182 = f32[256,2,2,32]{3,2,1,0:T(2,128)} reshape(f32[8,32,128]{2,1,0:T(8,128)} %shard_map.98) | data formatting | bytes 262144 | tf_op jit(solution)/shard_map/reshape | solution.py:625
  123.0 1.2 copy.41
  126.4 22.3 %shard_map.99 = f32[32,32,128]{2,1,0:T(8,128)} custom-call(f32[4,3,32,128]{3,2,1,0:T(8,128)} %get-tuple-element.11.refs_0_, f32[32,32,128]{2,1,0:T(8,128)} %add_divide_fusion.refs_1_, f32[4,2,32,128]{3,2,1,0:T(8,128)} %pad.4.refs_2_), custom_call_target="tpu_custom_call" | custom-call | tf_op jit(solution)/shard_map/pallas_call | solution.py:355
  148.7 1.4 slice_reduce_fusion
  150.1 1.2 fusion
  151.3 0.9 reshape_reshape.3.x_ref
  152.2 26.7 %shard_map.100 = f32[128,2,16]{2,1,0:T(2,128)} custom-call(f32[128,2,16]{2,1,0:T(2,128)} %reshape_reshape.3.x_ref), custom_call_target="tpu_custom_call" | custom-call | tf_op jit(solution)/shard_map/pallas_call | solution.py:435
  178.9 1.2 fusion.5
  182.0 1.7 copy.51
  (67 shorter events, 15.3 us)
Async XLA Ops:
  0.6 79.6 %copy-start = (f32[256,256]{1,0:T(8,128)S(1)}, f32[256,256]{1,0:T(8,128)}, u32[]{:S(2)}) copy-start(f32[256,256]{1,0:T(8,128)} %param.9) | copy-start | bytes 786436
  27.7 36.4 %copy-start.2 = (s32[4096]{0:T(1024)}, s32[4096]{0:T(1024)S(1)}, u32[]{:S(2)}) copy-start(s32[4096]{0:T(1024)S(1)} %add.192) | copy-start | bytes 49156
  27.8 38.1 %copy-start.3 = (s32[4096]{0:T(1024)}, s32[4096]{0:T(1024)S(1)}, u32[]{:S(2)}) copy-start(s32[4096]{0:T(1024)S(1)} %add.198) | copy-start | bytes 49156
  112.5 69.5 %copy-start.1 = (f32[6,32,32,128]{3,2,1,0:T(8,128)S(1)}, f32[6,32,32,128]{3,2,1,0:T(8,128)}, u32[]{:S(2)}) copy-start(f32[6,32,32,128]{3,2,1,0:T(8,128)} %get-tuple-element.28) | copy-start | bytes 9437188

commit v9 on v7

--- a/solution.py
+++ b/solution.py
@@ -384,7 +384,7 @@
     return tuple(coords[a] if a in coords else lax.axis_index(a) for a in ("gx", "gy"))
 
 
-def exchange(pieces, axes, gather, tag):
+def exchange(pieces, axes, gather, tag, summed=False):
     count, sizes = group_of(axes)
     piece_shape = pieces.shape if gather else pieces.shape[1:]
 
@@ -426,9 +426,30 @@
                 device_id_type=pl.DeviceIdType.MESH,
             ).wait_recv()
 
+    def summing_kernel(x_ref, s_ref, o_ref, send_sem, recv_sem):
+        kernel(x_ref, o_ref, send_sem, recv_sem)
+        total = o_ref[0]
+        for source in range(1, count):
+            total = total + o_ref[source]
+        s_ref[...] = total
+
+    gathered = jax.ShapeDtypeStruct((count,) + tuple(piece_shape), pieces.dtype)
+    if summed:
+        return pl.pallas_call(
+            summing_kernel,
+            out_shape=jax.ShapeDtypeStruct(tuple(piece_shape), pieces.dtype),
+            in_specs=[pl.BlockSpec(memory_space=pltpu.VMEM)],
+            out_specs=pl.BlockSpec(memory_space=pltpu.VMEM),
+            scratch_shapes=[
+                pltpu.VMEM(gathered.shape, pieces.dtype),
+                pltpu.SemaphoreType.DMA((count,)),
+                pltpu.SemaphoreType.DMA((count,)),
+            ],
+            compiler_params=pltpu.CompilerParams(collective_id=tag, has_side_effects=True),
+        )(pieces)
     return pl.pallas_call(
         kernel,
-        out_shape=jax.ShapeDtypeStruct((count,) + tuple(piece_shape), pieces.dtype),
+        out_shape=gathered,
         in_specs=[pl.BlockSpec(memory_space=pltpu.VMEM)],
         out_specs=pl.BlockSpec(memory_space=pltpu.VMEM),
         scratch_shapes=[pltpu.SemaphoreType.DMA((count,)), pltpu.SemaphoreType.DMA((count,))],
@@ -542,11 +563,11 @@
     offsets = jnp.arange(16, dtype=jnp.int32)
     capacity = 2 * max(1, P_DEV // devices)
     target_tile = pillar_tile[:, 0]
-    onehot = (target_tile[:, None] == jnp.arange(devices, dtype=jnp.int32)[None, :]).astype(
-        jnp.int32
-    )
-    earlier = jnp.cumsum(onehot, axis=0) - onehot
-    order_in = jnp.sum(earlier * onehot, axis=1)
+    pillar_index = jnp.arange(target_tile.shape[0], dtype=jnp.int32)
+    same_before = (target_tile[None, :] == target_tile[:, None]) & (
+        pillar_index[None, :] < pillar_index[:, None]
+    )
+    order_in = jnp.sum(same_before.astype(jnp.int32), axis=1)
     slot_ids = target_tile * capacity + order_in
     rows = jnp.concatenate(
         [intersection * widths[:, None], anchors.astype(jnp.float32)], axis=1
@@ -583,8 +604,8 @@
     )
     chunk_u = U // span_x
     part = part.reshape(2, span_x, chunk_u, 2, TILE).transpose(1, 2, 0, 3, 4)
-    part = exchange(part.reshape(span_x, chunk_u, 4 * TILE), ("gx",), False, 1)
-    part = jnp.sum(part, axis=0).reshape(chunk_u, 2, 2, TILE)
+    part = exchange(part.reshape(span_x, chunk_u, 4 * TILE), ("gx",), False, 1, summed=True)
+    part = part.reshape(chunk_u, 2, 2, TILE)
     part_re, part_im = part[:, 0], part[:, 1]
     far = jnp.stack(
         [

time: 181 us -> 180 us (level)
  other arithmetic: 11 us -> 9.18 us
where the time goes in v9:
time: 180 us
  Pallas kernels  147 us (82%)
  local copies, waits for them, and re-layouts  13.1 us (7%)
  other arithmetic  9.18 us (5%)
  matrix products  9.16 us (5%)
    pallas_call x2, Pallas kernels, run_leaps(): pl.pallas_call(kernel, out_shape=out_shape, in_specs=[pl.BlockSpec(memory...  57.3 us
    pallas_call x3, Pallas kernels, exchange(): pl.pallas_call(kernel, out_shape=gathered, in_specs=[pl.BlockSpec(memory_...  53.6 us
    pallas_call x1, Pallas kernels, focal_rows(): pl.pallas_call(kernel, out_shape=(jax.ShapeDtypeStruct((rows, width), jnp...  27.1 us
    pallas_call x1, Pallas kernels, exchange(): pl.pallas_call(summing_kernel, out_shape=jax.ShapeDtypeStruct(tuple(piece...  9.11 us
    dot_general x16, matrix products, contract(): jnp.einsum(pattern, first_op, second_op, precision=lax.Precision.HIGHEST)  7.66 us

profile of v9, /device:TPU:1, one launch (start us, length us, event | category | flops | bytes accessed | tf_op | source)
XLA Modules:
  0.0 179.7 jit_solution(9064345863064764812)
XLA Ops:
  0.6 0.9 convert_reduce_fusion
  2.2 0.7 broadcast_multiply_fusion
  3.6 1.0 fusion.13
  4.6 20.7 %shard_map.94 = f32[128,2,18]{2,1,0:T(2,128)} custom-call(f32[128,2,18]{2,1,0:T(2,128)} %bitcast.139), custom_call_target="tpu_custom_call" | custom-call | tf_op jit(solution)/shard_map/pallas_call | solution.py:450
  25.3 1.0 slice_convert_fusion
  26.9 1.0 mul.169
  28.4 2.0 %add_divide_fusion.refs_1_ = f32[32,32,128]{2,1,0:T(8,128)} fusion(f32[32,32,128]{2,1,0:T(8,128)} %param.8, f32[128]{0:T(128)S(1)} %and_convert_fusion, f32[32,32]{1,0:T(8,128)S(1)} %convolution_multiply_fusion), kind=kLoop, calls=%fused_computation.17 | loop fusion | flops 393216 | bytes 1053184 | tf_op jit(solution)/shard_map/div | solution.py:587
  30.5 33.6 %shard_map.95 = (f32[6,32,32,128]{3,2,1,0:T(8,128)}, f32[4,3,32,32,128]{4,3,2,1,0:T(8,128)}, f32[4,2,32,128]{3,2,1,0:T(8,128)}) custom-call(f32[6,32,32,128]{3,2,1,0:T(8,128)} %refs_0_.1, f32[32,32,128]{2,1,0:T(8,128)} %add_divide_fusion.refs_1_), custom_call_target="tpu_custom_call" | custom-call | tf_op jit(solution)/shard_map/pallas_call | solution.py:349
  64.0 0.9 slice_bitcast_fusion
  67.2 1.1 reshape.161.x_ref
  68.3 9.1 %shard_map.96 = f32[32,128]{1,0:T(8,128)} custom-call(f32[8,32,128]{2,1,0:T(8,128)} %reshape.161.x_ref), custom_call_target="tpu_custom_call" | custom-call | tf_op jit(solution)/shard_map/pallas_call | solution.py:438
  77.4 0.8 reshape.162
  80.2 0.7 reshape.163.x_ref
  81.5 27.1 %shard_map.97 = (f32[8,256]{1,0:T(8,128)}, f32[16,8,256]{2,1,0:T(8,128)}) custom-call(f32[16,8,256]{2,1,0:T(8,128)} %reshape.163.x_ref, f32[8,256]{1,0:T(8,128)} %reshape.164.t_ref), custom_call_target="tpu_custom_call" | custom-call | tf_op jit(solution)/shard_map/pallas_call | solution.py:515
  108.7 1.0 reshape.165
  111.5 0.7 reshape.167.x_ref
  112.2 6.7 %shard_map.98 = f32[8,32,128]{2,1,0:T(8,128)} custom-call(f32[32,128]{1,0:T(8,128)} %reshape.167.x_ref), custom_call_target="tpu_custom_call" | custom-call | tf_op jit(solution)/shard_map/pallas_call | solution.py:450
  118.9 1.3 reshape.183
  122.9 23.7 %shard_map.99 = f32[32,32,128]{2,1,0:T(8,128)} custom-call(f32[4,3,32,32,128]{4,3,2,1,0:T(8,128)} %get-tuple-element.11.refs_0_, f32[32,32,128]{2,1,0:T(8,128)} %add_divide_fusion.refs_1_, f32[4,2,32,128]{3,2,1,0:T(8,128)} %pad.4.refs_2_), custom_call_target="tpu_custom_call" | custom-call | tf_op jit(solution)/shard_map/pallas_call | solution.py:349
  146.7 1.4 slice_reduce_fusion
  148.6 0.9 reshape_reshape.3.x_ref
  149.4 26.2 %shard_map.100 = f32[128,2,16]{2,1,0:T(2,128)} custom-call(f32[128,2,16]{2,1,0:T(2,128)} %reshape_reshape.3.x_ref), custom_call_target="tpu_custom_call" | custom-call | tf_op jit(solution)/shard_map/pallas_call | solution.py:450
  175.6 1.2 fusion.5
  178.0 1.7 copy.53
  (64 shorter events, 13.0 us)
Async XLA Ops:
  0.6 80.3 %copy-start = (f32[256,256]{1,0:T(8,128)S(1)}, f32[256,256]{1,0:T(8,128)}, u32[]{:S(2)}) copy-start(f32[256,256]{1,0:T(8,128)} %param.9) | copy-start | bytes 786436
  122.9 52.7 %copy-start.3 = (f32[128,16]{0,1:T(8,128)S(1)}, f32[128,16]{0,1:T(8,128)}, u32[]{:S(2)}) copy-start(f32[128,16]{0,1:T(8,128)} %param.11) | copy-start | bytes 24580
  122.9 54.4 %copy-start.2 = (f32[8,256]{1,0:T(8,128)S(1)}, f32[8,256]{1,0:T(8,128)}, u32[]{:S(2)}) copy-start(f32[8,256]{1,0:T(8,128)} %get-tuple-element.10) | copy-start | bytes 24580
  122.9 55.1 %copy-start.1 = (f32[6,32,32,128]{3,2,1,0:T(8,128)S(1)}, f32[6,32,32,128]{3,2,1,0:T(8,128)}, u32[]{:S(2)}) copy-start(f32[6,32,32,128]{3,2,1,0:T(8,128)} %get-tuple-element.28) | copy-start | bytes 9437188

commit v10 on v9

--- a/solution.py
+++ b/solution.py
@@ -74,9 +74,9 @@
     def kernel(*refs):
         refs = list(refs)
         if adjoint:
-            hist, eps_ref, drv, acc = refs[:4]
-            a_hist, h_state = refs[4:6]
-            rest = refs[6:]
+            hist, eps_ref, drv, col_out = refs[:4]
+            a_hist, h_state, acc = refs[4:7]
+            rest = refs[7:]
         else:
             f_in, eps_ref, final, chg, mon = refs[:5]
             a_hist = refs[5]
@@ -276,7 +276,14 @@
                     + ez * hist[moment - 1, 2, x]
                 )
                 before = zero_slab if step == 0 else acc[x]
-                acc[x] = before - product * scale
+                total = before - product * scale
+                if step == NT - 1:
+                    pair = total + pltpu.roll(total, size_z - 1, 1)
+                    quad = pair + pltpu.roll(pair, size_z - 2, 1)
+                    moved = pltpu.roll(quad, (x - (ZM - ZP)) % size_z, 1)
+                    column[0] = jnp.where(iz == x, moved, column[0])
+                else:
+                    acc[x] = total
             else:
                 for comp, value in enumerate((ex, ey, ez)):
                     chg[step, comp, x] = value - e_old[comp]
@@ -290,6 +297,7 @@
                     xs_e[step + 1, 1] = ez
 
         packed = [zero_slab, zero_slab]
+        column = [zero_slab]
         for step in range(NT):
             skip_magnetic = adjoint and step == 0
             if not skip_magnetic:
@@ -325,17 +333,20 @@
 
         for copy, sends in sent:
             pl.when(sends)(copy.wait_send)
+        if adjoint:
+            col_out[...] = column[0]
 
     rim_x = pltpu.VMEM((NT, 2, size_y, size_z), jnp.float32)
     rim_y = pltpu.VMEM((NT, 2, 2, half, size_z), jnp.float32)
     field_shape = (size_x, size_y, size_z)
     if adjoint:
         operands = [history, inv_eps, drive]
-        out_shape = jax.ShapeDtypeStruct(field_shape, jnp.float32)
+        out_shape = jax.ShapeDtypeStruct((size_y, size_z), jnp.float32)
         out_specs = pl.BlockSpec(memory_space=pltpu.VMEM)
         state = [
             pltpu.VMEM((2, 3) + field_shape, jnp.float32),
             pltpu.VMEM((3,) + field_shape, jnp.float32),
+            pltpu.VMEM(field_shape, jnp.float32),
         ]
     else:
         operands = [fields, inv_eps]
@@ -655,9 +666,8 @@
         drives.append(adj_drive)
     drive = jnp.stack(drives).swapaxes(2, 3)
     drive = jnp.pad(drive, ((0, 0), (0, 0), (0, 0), (0, fields.shape[3] - TILE)))
-    grad_eps = run_leaps(None, inv_eps, e_changes, drive, 11)
-    column_grad = jnp.sum(grad_eps[:, :, ZM - ZP : ZM], axis=2)
-    spread = contract("sx,xy->sy", pick_x, column_grad)
+    column_grad_t = run_leaps(None, inv_eps, e_changes, drive, 11)[:, :TILE]
+    spread = contract("sx,yx->sy", pick_x, column_grad_t)
     picked = jnp.sum(spread * pick_y, axis=1).reshape(devices * capacity, 16)
     returned = exchange(picked.reshape(devices, capacity, 16), ("gx", "gy"), False, 5)
     own_vals = contract("ps,sk->pk", placing, returned.reshape(devices * capacity, 16))

time: 180 us -> 182 us (1.011)
  Pallas kernels: 147 us -> 150 us
where the time goes in v10:
time: 182 us; the launch traced here: 181 us
  Pallas kernels  150 us (82%)
  local copies, waits for them, and re-layouts  13 us (7%)
  matrix products  9.83 us (5%)
  other arithmetic  7.76 us (4%)
    pallas_call x2, Pallas kernels, run_leaps(): pl.pallas_call(kernel, out_shape=out_shape, in_specs=[pl.BlockSpec(memory...  58.6 us
    pallas_call x3, Pallas kernels, exchange(): pl.pallas_call(kernel, out_shape=gathered, in_specs=[pl.BlockSpec(memory_...  54.8 us
    pallas_call x1, Pallas kernels, focal_rows(): pl.pallas_call(kernel, out_shape=(jax.ShapeDtypeStruct((rows, width), jnp...  27.1 us
    pallas_call x1, Pallas kernels, exchange(): pl.pallas_call(summing_kernel, out_shape=jax.ShapeDtypeStruct(tuple(piece...  9.11 us
    dot_general x16, matrix products, contract(): jnp.einsum(pattern, first_op, second_op, precision=lax.Precision.HIGHEST)  8.33 us

profile of v10, /device:TPU:1, one launch (start us, length us, event | category | flops | bytes accessed | tf_op | source)
XLA Modules:
  0.0 181.4 jit_solution(11141176036422408069)
XLA Ops:
  0.6 0.9 convert_reduce_fusion
  2.2 0.7 broadcast_multiply_fusion
  3.6 1.0 fusion.13
  4.6 20.7 %shard_map.94 = f32[128,2,18]{2,1,0:T(2,128)} custom-call(f32[128,2,18]{2,1,0:T(2,128)} %bitcast.138), custom_call_target="tpu_custom_call" | custom-call | tf_op jit(solution)/shard_map/pallas_call | solution.py:461
  25.3 1.0 slice_convert_fusion
  26.9 1.0 mul.169
  28.4 2.0 %add_divide_fusion.refs_1_ = f32[32,32,128]{2,1,0:T(8,128)} fusion(f32[32,32,128]{2,1,0:T(8,128)} %param.8, f32[128]{0:T(128)S(1)} %and_convert_fusion, f32[32,32]{1,0:T(8,128)S(1)} %convolution_multiply_fusion), kind=kLoop, calls=%fused_computation.16 | loop fusion | flops 393216 | bytes 1053184 | tf_op jit(solution)/shard_map/div | solution.py:598
  30.5 33.6 %shard_map.95 = (f32[6,32,32,128]{3,2,1,0:T(8,128)}, f32[4,3,32,32,128]{4,3,2,1,0:T(8,128)}, f32[4,2,32,128]{3,2,1,0:T(8,128)}) custom-call(f32[6,32,32,128]{3,2,1,0:T(8,128)} %refs_0_.1, f32[32,32,128]{2,1,0:T(8,128)} %add_divide_fusion.refs_1_), custom_call_target="tpu_custom_call" | custom-call | tf_op jit(solution)/shard_map/pallas_call | solution.py:360
  64.0 0.9 slice_bitcast_fusion
  67.2 1.1 reshape.161.x_ref
  68.3 9.1 %shard_map.96 = f32[32,128]{1,0:T(8,128)} custom-call(f32[8,32,128]{2,1,0:T(8,128)} %reshape.161.x_ref), custom_call_target="tpu_custom_call" | custom-call | tf_op jit(solution)/shard_map/pallas_call | solution.py:449
  77.4 0.8 reshape.162
  80.2 0.7 reshape.163.x_ref
  81.5 27.1 %shard_map.97 = (f32[8,256]{1,0:T(8,128)}, f32[16,8,256]{2,1,0:T(8,128)}) custom-call(f32[16,8,256]{2,1,0:T(8,128)} %reshape.163.x_ref, f32[8,256]{1,0:T(8,128)} %reshape.164.t_ref), custom_call_target="tpu_custom_call" | custom-call | tf_op jit(solution)/shard_map/pallas_call | solution.py:526
  108.7 1.0 reshape.165
  111.5 0.7 reshape.167.x_ref
  112.2 6.7 %shard_map.98 = f32[8,32,128]{2,1,0:T(8,128)} custom-call(f32[32,128]{1,0:T(8,128)} %reshape.167.x_ref), custom_call_target="tpu_custom_call" | custom-call | tf_op jit(solution)/shard_map/pallas_call | solution.py:461
  118.9 1.3 reshape.183
  122.9 25.0 %shard_map.99 = f32[32,128]{1,0:T(8,128)} custom-call(f32[4,3,32,32,128]{4,3,2,1,0:T(8,128)} %get-tuple-element.11.refs_0_, f32[32,32,128]{2,1,0:T(8,128)} %add_divide_fusion.refs_1_, f32[4,2,32,128]{3,2,1,0:T(8,128)} %pad.4.refs_2_), custom_call_target="tpu_custom_call" | custom-call | tf_op jit(solution)/shard_map/pallas_call | solution.py:360
  148.0 1.1 fusion
  149.1 0.9 reshape_reshape.3.x_ref
  150.0 27.4 %shard_map.100 = f32[128,2,16]{2,1,0:T(2,128)} custom-call(f32[128,2,16]{2,1,0:T(2,128)} %reshape_reshape.3.x_ref), custom_call_target="tpu_custom_call" | custom-call | tf_op jit(solution)/shard_map/pallas_call | solution.py:461
  177.4 1.2 fusion.5
  179.7 1.7 copy.53
  (63 shorter events, 12.6 us)
Async XLA Ops:
  0.6 80.3 %copy-start = (f32[256,256]{1,0:T(8,128)S(1)}, f32[256,256]{1,0:T(8,128)}, u32[]{:S(2)}) copy-start(f32[256,256]{1,0:T(8,128)} %param.9) | copy-start | bytes 786436
  122.9 54.4 %copy-start.3 = (f32[128,16]{0,1:T(8,128)S(1)}, f32[128,16]{0,1:T(8,128)}, u32[]{:S(2)}) copy-start(f32[128,16]{0,1:T(8,128)} %param.11) | copy-start | bytes 24580
  122.9 56.2 %copy-start.2 = (f32[8,256]{1,0:T(8,128)S(1)}, f32[8,256]{1,0:T(8,128)}, u32[]{:S(2)}) copy-start(f32[8,256]{1,0:T(8,128)} %get-tuple-element.10) | copy-start | bytes 24580
  122.9 56.8 %copy-start.1 = (f32[6,32,32,128]{3,2,1,0:T(8,128)S(1)}, f32[6,32,32,128]{3,2,1,0:T(8,128)}, u32[]{:S(2)}) copy-start(f32[6,32,32,128]{3,2,1,0:T(8,128)} %get-tuple-element.28) | copy-start | bytes 9437188

commit v11 on v9

--- a/solution.py
+++ b/solution.py
@@ -640,10 +640,10 @@
     half = half.reshape(span_x * chunk_u, 2, 2, TILE).transpose(1, 2, 0, 3)
     half_re, half_im = half[0], half[1]
     back_re = 2.0 * norm_scale * (
-        contract("ux,cuy->cxy", x_re, half_re) - contract("ux,cuy->cxy", x_im, half_im)
+        contract("ux,cuy->cyx", x_re, half_re) - contract("ux,cuy->cyx", x_im, half_im)
     )
     back_im = 2.0 * norm_scale * (
-        contract("ux,cuy->cxy", x_re, half_im) + contract("ux,cuy->cxy", x_im, half_re)
+        contract("ux,cuy->cyx", x_re, half_im) + contract("ux,cuy->cyx", x_im, half_re)
     )
     drives = []
     for moment in range(1, NT + 1):
@@ -653,7 +653,7 @@
             + math.sin(ANGULAR_STEP * source_step) * back_im
         )
         drives.append(adj_drive)
-    drive = jnp.stack(drives).swapaxes(2, 3)
+    drive = jnp.stack(drives)
     drive = jnp.pad(drive, ((0, 0), (0, 0), (0, 0), (0, fields.shape[3] - TILE)))
     grad_eps = run_leaps(None, inv_eps, e_changes, drive, 11)
     column_grad = jnp.sum(grad_eps[:, :, ZM - ZP : ZM], axis=2)

time: 180 us -> 180 us (level)
  no operation moved by 1% of the time
where the time goes in v11:
time: 180 us
  Pallas kernels  147 us (82%)
  local copies, waits for them, and re-layouts  12.4 us (7%)
  other arithmetic  9.84 us (5%)
  matrix products  9.16 us (5%)
    pallas_call x2, Pallas kernels, run_leaps(): pl.pallas_call(kernel, out_shape=out_shape, in_specs=[pl.BlockSpec(memory...  57.3 us
    pallas_call x3, Pallas kernels, exchange(): pl.pallas_call(kernel, out_shape=gathered, in_specs=[pl.BlockSpec(memory_...  53.6 us
    pallas_call x1, Pallas kernels, focal_rows(): pl.pallas_call(kernel, out_shape=(jax.ShapeDtypeStruct((rows, width), jnp...  27.1 us
    pallas_call x1, Pallas kernels, exchange(): pl.pallas_call(summing_kernel, out_shape=jax.ShapeDtypeStruct(tuple(piece...  9.11 us
    dot_general x16, matrix products, contract(): jnp.einsum(pattern, first_op, second_op, precision=lax.Precision.HIGHEST)  7.66 us

profile of v11, /device:TPU:1, one launch (start us, length us, event | category | flops | bytes accessed | tf_op | source)
XLA Modules:
  0.0 179.7 jit_solution(11363737804820886812)
XLA Ops:
  0.6 0.9 convert_reduce_fusion
  2.2 0.7 broadcast_multiply_fusion
  3.6 1.0 fusion.13
  4.6 20.7 %shard_map.94 = f32[128,2,18]{2,1,0:T(2,128)} custom-call(f32[128,2,18]{2,1,0:T(2,128)} %bitcast.129), custom_call_target="tpu_custom_call" | custom-call | tf_op jit(solution)/shard_map/pallas_call | solution.py:450
  25.3 1.0 slice_convert_fusion
  26.9 1.0 mul.161
  28.4 2.0 %add_divide_fusion.refs_1_ = f32[32,32,128]{2,1,0:T(8,128)} fusion(f32[32,32,128]{2,1,0:T(8,128)} %param.8, f32[128]{0:T(128)S(1)} %and_convert_fusion, f32[32,32]{1,0:T(8,128)S(1)} %convolution_multiply_fusion), kind=kLoop, calls=%fused_computation.17 | loop fusion | flops 393216 | bytes 1053184 | tf_op jit(solution)/shard_map/div | solution.py:587
  30.5 33.6 %shard_map.95 = (f32[6,32,32,128]{3,2,1,0:T(8,128)}, f32[4,3,32,32,128]{4,3,2,1,0:T(8,128)}, f32[4,2,32,128]{3,2,1,0:T(8,128)}) custom-call(f32[6,32,32,128]{3,2,1,0:T(8,128)} %refs_0_.1, f32[32,32,128]{2,1,0:T(8,128)} %add_divide_fusion.refs_1_), custom_call_target="tpu_custom_call" | custom-call | tf_op jit(solution)/shard_map/pallas_call | solution.py:349
  64.0 0.9 slice_bitcast_fusion
  67.2 1.1 reshape.161.x_ref
  68.3 9.1 %shard_map.96 = f32[32,128]{1,0:T(8,128)} custom-call(f32[8,32,128]{2,1,0:T(8,128)} %reshape.161.x_ref), custom_call_target="tpu_custom_call" | custom-call | tf_op jit(solution)/shard_map/pallas_call | solution.py:438
  77.4 0.8 reshape.162
  80.2 0.7 reshape.163.x_ref
  81.5 27.1 %shard_map.97 = (f32[8,256]{1,0:T(8,128)}, f32[16,8,256]{2,1,0:T(8,128)}) custom-call(f32[16,8,256]{2,1,0:T(8,128)} %reshape.163.x_ref, f32[8,256]{1,0:T(8,128)} %reshape.164.t_ref), custom_call_target="tpu_custom_call" | custom-call | tf_op jit(solution)/shard_map/pallas_call | solution.py:515
  108.7 1.0 reshape.165
  111.5 0.7 reshape.167.x_ref
  112.2 6.7 %shard_map.98 = f32[8,32,128]{2,1,0:T(8,128)} custom-call(f32[32,128]{1,0:T(8,128)} %reshape.167.x_ref), custom_call_target="tpu_custom_call" | custom-call | tf_op jit(solution)/shard_map/pallas_call | solution.py:450
  118.9 1.3 reshape.183
  122.9 23.7 %shard_map.99 = f32[32,32,128]{2,1,0:T(8,128)} custom-call(f32[4,3,32,32,128]{4,3,2,1,0:T(8,128)} %get-tuple-element.11.refs_0_, f32[32,32,128]{2,1,0:T(8,128)} %add_divide_fusion.refs_1_, f32[4,2,32,128]{3,2,1,0:T(8,128)} %select_maximum_fusion.refs_2_), custom_call_target="tpu_custom_call" | custom-call | tf_op jit(solution)/shard_map/pallas_call | solution.py:349
  146.7 1.4 slice_reduce_fusion
  148.5 0.9 reshape_reshape.3.x_ref
  149.4 26.2 %shard_map.100 = f32[128,2,16]{2,1,0:T(2,128)} custom-call(f32[128,2,16]{2,1,0:T(2,128)} %reshape_reshape.3.x_ref), custom_call_target="tpu_custom_call" | custom-call | tf_op jit(solution)/shard_map/pallas_call | solution.py:450
  175.6 1.2 fusion.5
  178.0 1.7 copy.53
  (63 shorter events, 13.0 us)
Async XLA Ops:
  0.6 80.3 %copy-start = (f32[256,256]{1,0:T(8,128)S(1)}, f32[256,256]{1,0:T(8,128)}, u32[]{:S(2)}) copy-start(f32[256,256]{1,0:T(8,128)} %param.9) | copy-start | bytes 786436
  122.9 52.7 %copy-start.3 = (f32[128,16]{0,1:T(8,128)S(1)}, f32[128,16]{0,1:T(8,128)}, u32[]{:S(2)}) copy-start(f32[128,16]{0,1:T(8,128)} %param.11) | copy-start | bytes 24580
  122.9 54.4 %copy-start.2 = (f32[8,256]{1,0:T(8,128)S(1)}, f32[8,256]{1,0:T(8,128)}, u32[]{:S(2)}) copy-start(f32[8,256]{1,0:T(8,128)} %get-tuple-element.10) | copy-start | bytes 24580
  122.9 55.1 %copy-start.1 = (f32[6,32,32,128]{3,2,1,0:T(8,128)S(1)}, f32[6,32,32,128]{3,2,1,0:T(8,128)}, u32[]{:S(2)}) copy-start(f32[6,32,32,128]{3,2,1,0:T(8,128)} %get-tuple-element.28) | copy-start | bytes 9437188
